TPU v7x, 32 devices: a whole 2x2x4 slice. The times are simulated.
32 devices in a mesh: dp: 8 (over z, x), expert: 4 (over y, core).
Axes of the slice: x: 2, y: 2, z: 4, core: 2. Of those that a mesh axis runs over, the one named last changes fastest.
Arguments:
- layer_input: bfloat16 [8192, 768], P(('dp', 'expert')), may hold values from -6 to 6
- output_grad: bfloat16 [8192, 768], P(('dp', 'expert')), may hold values from -6 to 6
- prev_logits: bfloat16 [8192, 12], P(('dp', 'expert')), may hold values from -3 to 3
- deal_order: int32 [8, 1024], P('dp', 'expert'), may hold values from 0 to 1023, each once within a row
- routes: int32 [8192, 2], P(('dp', 'expert')), may hold values from 0 to 11, all different within a row; in each aligned block of 256 rows (0 to 255, 256 to 511, ...) at most 64 rows name the same one
- lengths: int32 [32], P(('dp', 'expert')), may hold values from 1 to 256, 6144 in all
- attention_gain: float32 [768], replicated, may hold values from 0.1 to 1.9
- mixture_gain: float32 [768], replicated, may hold values from 0.1 to 1.9
- attention_in: bfloat16 [768, 2304], replicated, may hold values from -0.21875 to 0.21875
- attention_out: bfloat16 [768, 768], replicated, may hold values from -1.75 to 1.75
- router_weight: bfloat16 [768, 12], replicated, may hold values from -0.15625 to 0.15625
- constant_mix: bfloat16 [768, 4], replicated, may hold values from -0.15625 to 0.15625
- constant_value: bfloat16 [768, 2], replicated, may hold values from -4 to 4
- expert_gate_up: bfloat16 [8, 768, 4096], P('expert'), may hold values from -0.21875 to 0.21875
- expert_down: bfloat16 [8, 2048, 768], P('expert'), may hold values from -0.25 to 0.25
Outputs:
- layer_output: bfloat16 [8192, 768], P(('dp', 'expert'))
- input_grad: bfloat16 [8192, 768], P(('dp', 'expert'))
- prev_grad: bfloat16 [8192, 12], P(('dp', 'expert'))
- attention_gain_grad: float32 [768], P('dp')
- mixture_gain_grad: float32 [768], P('dp')
- attention_in_grad: float32 [768, 2304], P('dp')
- attention_out_grad: float32 [768, 768], P('dp')
- router_grad: float32 [768, 12], P('dp')
- constant_mix_grad: float32 [768, 4], P('dp')
- constant_value_grad: float32 [768, 2], P('dp')
- gate_up_grad: float32 [8, 768, 4096], P('expert', 'dp')
- down_grad: float32 [8, 2048, 768], P('expert', 'dp')
Inputs may be any that keep to these rules, and one draw needn't show every extreme that they name: `routes`: each token names two different choices; among the rows of one device no choice is named by more than 64 rows, a bound that some block reaches. `deal_order`: each row is a permutation of 0 to 1023. `lengths`: they sum to 6144 and the longest is 256.
All inputs are finite; a program needn't handle non-finite values. No bound on the sum of `lengths` on one device may be relied on, other than what follows from the above.
Results may differ from a plain program's by a relative error of at most 0.017.
Values may be sent and summed in bfloat16 or wider, within the bound.
No kernel may reach another device: no remote copies, remote signals or barrier semaphores. Data moves between devices by JAX's collectives and lax.ppermute only.
A program may use at most 192 MiB of HBM per device.

v0:
```python
import jax
import jax.numpy as jnp
from jax import lax
from jax.sharding import PartitionSpec as P

HEADS = 12


epsilon = 1e-06
rope_base = 10000.0
highest = lax.Precision.HIGHEST


def norm_forward(values, norm_gain):
    inverse = lax.rsqrt(jnp.mean(values * values, axis=-1, keepdims=True) + epsilon)
    unit_rows = values * inverse
    return (unit_rows * norm_gain, unit_rows, inverse)


def norm_backward(upstream, unit_rows, inverse, norm_gain):
    scaled = upstream * norm_gain
    gain_grad = jnp.sum(upstream * unit_rows, axis=0)
    back_rows = inverse * (
        scaled - unit_rows * jnp.mean(scaled * unit_rows, axis=-1, keepdims=True)
    )
    return (back_rows, gain_grad)


def rope_tables(count, half_size):
    positions = jnp.arange(count, dtype=jnp.float32)
    inverse_freq = rope_base ** (-jnp.arange(half_size, dtype=jnp.float32) / half_size)
    angles = positions[:, None] * inverse_freq[None, :]
    return (jnp.cos(angles)[:, None, :], jnp.sin(angles)[:, None, :])


def rotate_forward(values, cosine_table, sine_table):
    half_size = values.shape[-1] // 2
    first_half = values[..., :half_size]
    second_half = values[..., half_size:]
    return jnp.concatenate(
        [
            first_half * cosine_table - second_half * sine_table,
            second_half * cosine_table + first_half * sine_table,
        ],
        axis=-1,
    )


def rotate_backward(values, cosine_table, sine_table):
    half_size = values.shape[-1] // 2
    first_half = values[..., :half_size]
    second_half = values[..., half_size:]
    return jnp.concatenate(
        [
            first_half * cosine_table + second_half * sine_table,
            second_half * cosine_table - first_half * sine_table,
        ],
        axis=-1,
    )


def local(
    layer_input,
    output_grad,
    prev_logits,
    deal_order,
    routes,
    lengths,
    attention_gain,
    mixture_gain,
    attention_in,
    attention_out,
    router_weight,
    constant_mix,
    constant_value,
    expert_gate_up,
    expert_down,
):
    tok_count = layer_input.shape[0]
    model_width = layer_input.shape[1]
    choice_count = prev_logits.shape[1]
    local_experts = expert_gate_up.shape[0]
    hidden_units = expert_down.shape[1]
    peer_count = lax.axis_size("expert")
    experts_all = local_experts * peer_count
    capacity = tok_count // 4
    head_count = HEADS
    head_size = model_width // head_count
    half_size = head_size // 2
    score_scale = head_size ** (-0.5)
    slot_order = deal_order[0]
    group_x, group_prev = (
        lax.all_gather(layer_input, "expert", axis=0, tiled=True),
        lax.all_gather(prev_logits, "expert", axis=0, tiled=True),
    )
    group_rows = group_x.shape[0]
    dealt_rows = group_x[slot_order].astype(jnp.float32)
    prev_dealt = group_prev[slot_order].astype(jnp.float32)
    normed_first, unit_first, inverse_first = norm_forward(dealt_rows, attention_gain)
    first_low = normed_first.astype(jnp.bfloat16)
    projected = jnp.dot(first_low, attention_in, preferred_element_type=jnp.float32)
    projected = projected.reshape(tok_count, 3, head_count, head_size)
    cosine_table, sine_table = rope_tables(tok_count, half_size)
    query_rot = rotate_forward(projected[:, 0], cosine_table, sine_table).astype(jnp.bfloat16)
    key_rot = rotate_forward(projected[:, 1], cosine_table, sine_table).astype(jnp.bfloat16)
    value_low = projected[:, 2].astype(jnp.bfloat16)
    position = jnp.arange(tok_count, dtype=jnp.int32)
    allowed = (position[None, :] <= position[:, None]) & (position[None, :] < lengths[0])

    def score_block(query_part, key_part):
        raw_scores = (
            jnp.einsum("ihd,jhd->hij", query_part, key_part, preferred_element_type=jnp.float32)
            * score_scale
        )
        return jnp.where(allowed[None], raw_scores, -jnp.inf)

    scores = score_block(query_rot, key_rot)
    score_peak = jnp.max(scores, axis=-1, keepdims=True)
    exp_scores = jnp.exp(scores - score_peak)
    exp_total = jnp.sum(exp_scores, axis=-1, keepdims=True)
    score_probs = exp_scores / exp_total
    log_total = score_peak + jnp.log(exp_total)
    attended = (
        jnp.einsum(
            "hij,jhd->ihd",
            score_probs.astype(jnp.bfloat16),
            value_low,
            preferred_element_type=jnp.float32,
        )
        .astype(jnp.bfloat16)
        .reshape(tok_count, model_width)
    )
    residual = dealt_rows + jnp.dot(attended, attention_out, preferred_element_type=jnp.float32)
    normed_second, unit_second, inverse_second = norm_forward(residual, mixture_gain)
    second_low = normed_second.astype(jnp.bfloat16)
    logits = jnp.dot(second_low, router_weight, preferred_element_type=jnp.float32) + prev_dealt
    route_onehot = (routes[..., None] == jnp.arange(choice_count, dtype=jnp.int32)).astype(
        jnp.float32
    )
    picked = jnp.sum(route_onehot * logits[:, None, :], axis=-1)
    gate_values = jax.nn.softmax(picked, axis=-1)
    mix_logits = jnp.dot(second_low, constant_mix, preferred_element_type=jnp.float32).reshape(
        tok_count, 2, 2
    )
    mix_weights = jax.nn.softmax(mix_logits, axis=-1)
    const_rows = constant_value.astype(jnp.float32).T
    const_out = (
        mix_weights[:, :, 0:1] * normed_second[:, None, :]
        + mix_weights[:, :, 1:2] * const_rows[None]
    )
    flat_routes = routes.reshape(-1)
    flat_onehot = (
        flat_routes[:, None] == jnp.arange(choice_count, dtype=jnp.int32)[None, :]
    ).astype(jnp.int32)
    route_rank = jnp.sum((jnp.cumsum(flat_onehot, axis=0) - 1) * flat_onehot, axis=1)
    is_ffn = flat_routes < experts_all
    target = jnp.where(is_ffn, flat_routes * capacity + route_rank, experts_all * capacity)
    slot_route = jnp.full((experts_all * capacity + 1,), 2 * tok_count, jnp.int32)
    slot_route = slot_route.at[target].set(jnp.arange(2 * tok_count, dtype=jnp.int32))[
        : experts_all * capacity
    ]
    slot_token = slot_route // 2
    padded_input = jnp.concatenate([second_low, jnp.zeros((1, model_width), jnp.bfloat16)], axis=0)
    outgoing = padded_input[slot_token].reshape(peer_count, local_experts, capacity, model_width)
    incoming = lax.all_to_all(outgoing, "expert", split_axis=0, concat_axis=0, tiled=True)
    gate_up = jnp.einsum(
        "pecd,edf->pecf", incoming, expert_gate_up, preferred_element_type=jnp.float32
    )
    inner_low = (jax.nn.silu(gate_up[..., :hidden_units]) * gate_up[..., hidden_units:]).astype(
        jnp.bfloat16
    )
    produced = jnp.einsum(
        "pecf,efd->pecd", inner_low, expert_down, preferred_element_type=jnp.float32
    ).astype(jnp.bfloat16)
    sent_back = lax.all_to_all(produced, "expert", split_axis=0, concat_axis=0, tiled=True)
    returned_flat = sent_back.reshape(experts_all * capacity, model_width)
    safe_target = jnp.where(is_ffn, target, 0)
    route_out = returned_flat[safe_target].reshape(tok_count, 2, model_width).astype(jnp.float32)
    ffn_mask = (routes < experts_all)[..., None]
    copy_mask = routes == experts_all + 1
    const_mask = (
        routes[..., None] == (experts_all + 2 + jnp.arange(2, dtype=jnp.int32))[None, None, :]
    )
    branch = (
        jnp.where(ffn_mask, route_out, 0.0)
        + jnp.where(copy_mask[..., None], normed_second[:, None, :], 0.0)
        + jnp.where(const_mask[..., 0:1], const_out[:, 0][:, None, :], 0.0)
        + jnp.where(const_mask[..., 1:2], const_out[:, 1][:, None, :], 0.0)
    )
    output = residual + jnp.sum(gate_values[..., None] * branch, axis=1)
    placed_out = (
        jnp.zeros((group_rows, model_width), jnp.bfloat16)
        .at[slot_order]
        .set(output.astype(jnp.bfloat16))
    )
    out_rows = lax.psum_scatter(
        placed_out.astype(jnp.float32).astype(jnp.bfloat16),
        "expert",
        scatter_dimension=0,
        tiled=True,
    )
    group_dy = lax.all_gather(output_grad, "expert", axis=0, tiled=True)
    grad_out = group_dy[slot_order].astype(jnp.float32)
    weighted = gate_values[..., None] * grad_out[:, None, :]
    grad_gate = jnp.sum(branch * grad_out[:, None, :], axis=-1)
    grad_picked = gate_values * (
        grad_gate - jnp.sum(gate_values * grad_gate, axis=-1, keepdims=True)
    )
    grad_logits = jnp.sum(route_onehot * grad_picked[..., None], axis=1)
    padded_grad = jnp.concatenate(
        [
            weighted.reshape(2 * tok_count, model_width).astype(jnp.bfloat16),
            jnp.zeros((1, model_width), jnp.bfloat16),
        ],
        axis=0,
    )
    grad_send = padded_grad[slot_route].reshape(peer_count, local_experts, capacity, model_width)
    grad_recv = lax.all_to_all(grad_send, "expert", split_axis=0, concat_axis=0, tiled=True)
    gate_up = jnp.einsum(
        "pecd,edf->pecf", incoming, expert_gate_up, preferred_element_type=jnp.float32
    )
    gate_part = gate_up[..., :hidden_units]
    up_part = gate_up[..., hidden_units:]
    silu_gate = jax.nn.silu(gate_part)
    inner_low = (silu_gate * up_part).astype(jnp.bfloat16)
    down_partial = jnp.einsum(
        "pecf,pecd->efd", inner_low, grad_recv, preferred_element_type=jnp.float32
    )
    grad_inner = jnp.einsum(
        "pecd,efd->pecf", grad_recv, expert_down, preferred_element_type=jnp.float32
    )
    sigmoid_gate = jax.nn.sigmoid(gate_part)
    grad_gate_part = grad_inner * up_part * sigmoid_gate * (1.0 + gate_part * (1.0 - sigmoid_gate))
    grad_up_part = grad_inner * silu_gate
    grad_gate_up = jnp.concatenate([grad_gate_part, grad_up_part], axis=-1).astype(jnp.bfloat16)
    up_partial = jnp.einsum(
        "pecd,pecf->edf", incoming, grad_gate_up, preferred_element_type=jnp.float32
    )
    grad_rows = jnp.einsum(
        "pecf,edf->pecd", grad_gate_up, expert_gate_up, preferred_element_type=jnp.float32
    ).astype(jnp.bfloat16)
    grad_back = lax.all_to_all(grad_rows, "expert", split_axis=0, concat_axis=0, tiled=True)
    gate_up_sum, down_sum = (
        lax.psum_scatter(
            up_partial.astype(jnp.bfloat16), "dp", scatter_dimension=1, tiled=True
        ).astype(jnp.float32),
        lax.psum_scatter(
            down_partial.astype(jnp.bfloat16), "dp", scatter_dimension=1, tiled=True
        ).astype(jnp.float32),
    )
    back_flat = grad_back.reshape(experts_all * capacity, model_width)
    route_grad = back_flat[safe_target].reshape(tok_count, 2, model_width).astype(jnp.float32)
    expert_input_grad = jnp.sum(jnp.where(ffn_mask, route_grad, 0.0), axis=1)
    const_weight = jnp.sum(jnp.where(const_mask, gate_values[..., None], 0.0), axis=1)
    copy_weight = jnp.sum(jnp.where(copy_mask, gate_values, 0.0), axis=1)
    along_normed = jnp.sum(grad_out * normed_second, axis=-1)
    along_value = jnp.dot(grad_out, constant_value.astype(jnp.float32), precision=highest)
    grad_mix = jnp.stack(
        [const_weight * along_normed[:, None], const_weight * along_value], axis=-1
    )
    grad_mixlog = mix_weights * (grad_mix - jnp.sum(mix_weights * grad_mix, axis=-1, keepdims=True))
    grad_mixlog = grad_mixlog.reshape(tok_count, 4)
    value_grad = jnp.dot(grad_out.T, const_weight * mix_weights[:, :, 1], precision=highest)
    second_wide = second_low.astype(jnp.float32)
    mix_grad = jnp.dot(second_wide.T, grad_mixlog, precision=highest)
    router_partial = jnp.dot(second_wide.T, grad_logits, precision=highest)
    direct_scale = copy_weight + jnp.sum(const_weight * mix_weights[:, :, 0], axis=1)
    grad_second = (
        direct_scale[:, None] * grad_out
        + expert_input_grad
        + jnp.dot(grad_mixlog, constant_mix.astype(jnp.float32).T, precision=highest)
        + jnp.dot(grad_logits, router_weight.astype(jnp.float32).T, precision=highest)
    )
    back_second, gain_second = norm_backward(grad_second, unit_second, inverse_second, mixture_gain)
    grad_residual = grad_out + back_second
    grad_attn = grad_residual.astype(jnp.bfloat16)
    out_partial = jnp.dot(attended.T, grad_attn, preferred_element_type=jnp.float32)
    grad_attended = jnp.dot(grad_attn, attention_out.T, preferred_element_type=jnp.float32)
    grad_attended = grad_attended.astype(jnp.bfloat16).reshape(tok_count, head_count, head_size)
    probs_again = jnp.where(
        allowed[None], jnp.exp(score_block(query_rot, key_rot) - log_total), 0.0
    )
    grad_value = jnp.einsum(
        "hij,ihd->jhd",
        probs_again.astype(jnp.bfloat16),
        grad_attended,
        preferred_element_type=jnp.float32,
    )
    grad_probs = jnp.einsum(
        "ihd,jhd->hij", grad_attended, value_low, preferred_element_type=jnp.float32
    )
    grad_scores = (
        probs_again * (grad_probs - jnp.sum(probs_again * grad_probs, axis=-1, keepdims=True))
    ).astype(jnp.bfloat16)
    grad_query = (
        jnp.einsum("hij,jhd->ihd", grad_scores, key_rot, preferred_element_type=jnp.float32)
        * score_scale
    )
    grad_key = (
        jnp.einsum("hij,ihd->jhd", grad_scores, query_rot, preferred_element_type=jnp.float32)
        * score_scale
    )
    grad_qkv = jnp.stack(
        [
            rotate_backward(grad_query, cosine_table, sine_table),
            rotate_backward(grad_key, cosine_table, sine_table),
            grad_value,
        ],
        axis=1,
    )
    grad_qkv = grad_qkv.reshape(tok_count, 3 * model_width).astype(jnp.bfloat16)
    in_partial = jnp.dot(first_low.T, grad_qkv, preferred_element_type=jnp.float32)
    grad_first = jnp.dot(grad_qkv, attention_in.T, preferred_element_type=jnp.float32)
    back_first, gain_first = norm_backward(grad_first, unit_first, inverse_first, attention_gain)
    grad_dealt = grad_residual + back_first
    placed_x = (
        jnp.zeros((group_rows, model_width), jnp.bfloat16)
        .at[slot_order]
        .set(grad_dealt.astype(jnp.bfloat16))
    )
    placed_prev = (
        jnp.zeros((group_rows, choice_count), jnp.bfloat16)
        .at[slot_order]
        .set(grad_logits.astype(jnp.bfloat16))
    )
    input_rows, prev_rows = (
        lax.psum_scatter(
            placed_x.astype(jnp.float32).astype(jnp.bfloat16),
            "expert",
            scatter_dimension=0,
            tiled=True,
        ).astype(jnp.float32),
        lax.psum_scatter(
            placed_prev.astype(jnp.float32).astype(jnp.bfloat16),
            "expert",
            scatter_dimension=0,
            tiled=True,
        ).astype(jnp.float32),
    )
    totals = lax.psum(
        (gain_first, gain_second, in_partial, out_partial, router_partial, mix_grad, value_grad),
        ("dp", "expert"),
    )
    share_rows = model_width // lax.axis_size("dp")
    start_row = lax.axis_index("dp") * share_rows
    summed = tuple(
        (lax.dynamic_slice_in_dim(member, start_row, share_rows, 0) for member in totals)
    )
    return (
        out_rows,
        input_rows.astype(jnp.bfloat16),
        prev_rows.astype(jnp.bfloat16),
        summed[0],
        summed[1],
        summed[2],
        summed[3],
        summed[4],
        summed[5],
        summed[6],
        gate_up_sum,
        down_sum,
    )


def solution(mesh):
    in_specs = (
        P(("dp", "expert"), None),
        P(("dp", "expert"), None),
        P(("dp", "expert"), None),
        P("dp", "expert"),
        P(("dp", "expert"), None),
        P(("dp", "expert")),
        P(),
        P(),
        P(),
        P(),
        P(),
        P(),
        P(),
        P("expert", None, None),
        P("expert", None, None),
    )
    out_specs = (
        P(("dp", "expert"), None),
        P(("dp", "expert"), None),
        P(("dp", "expert"), None),
        P("dp"),
        P("dp"),
        P("dp", None),
        P("dp", None),
        P("dp", None),
        P("dp", None),
        P("dp", None),
        P("expert", "dp", None),
        P("expert", "dp", None),
    )
    return jax.shard_map(local, mesh=mesh, in_specs=in_specs, out_specs=out_specs, check_vma=False)
```

profile of v0, /device:TPU:0, one launch (start us, length us, event | category | flops | bytes accessed | tf_op | source)
XLA Modules:
  0.0 876.6 jit_solution(15144061251654223362)
XLA Ops:
  26.1 3.1 reduce-window.6
  34.2 2.6 scatter_custom_fusion
  38.9 10.7 %all_gather.10 = bf16[1024,12]{1,0:T(8,128)(2,1)} all-gather(bf16[256,12]{1,0:T(8,128)(2,1)} %copy.120), channel_id=1, replica_groups=mesh['dp'=8,'expert'=4] {'expert'}, dimensions={0}, use_global_device_ids=true | all-gather | bytes 30720 | tf_op jit(solution)/shard_map/all_gather | solution.py:94
  49.5 2.3 gather_fusion.1
  58.0 3.8 gather_fusion
  63.0 2.6 fusion.80
  72.0 3.9 gather_fusion.4
  77.8 2.1 multiply_reduce_fusion.5
  81.6 4.3 gather_fusion.2
  85.9 15.0 %all-to-all-start = ((bf16[4,2,64,768]{3,2,1,0:T(8,128)(2,1)}), bf16[4,2,64,768]{3,2,1,0:T(8,128)(2,1)}, u32[]{:S(2)}, u32[]{:S(2)}) async-start(bf16[4,2,64,768]{3,2,1,0:T(8,128)(2,1)} %bitcast.161), calls=%async_computation | async-start | bytes 1572864 | tf_op jit(solution)/shard_map/all_to_all | solution.py:165
  100.9 2.5 mul.575
  103.4 3.2 mul.576
  128.6 4.5 gather_fusion.5
  136.4 2.8 multiply_add_fusion
  139.2 4.2 all-to-all-start.2
  143.4 11.5 %fusion.4 = f32[4,2,64,4096]{3,2,0,1:T(8,128)} fusion(bf16[2,768,4096]{2,1,0:T(8,128)(2,1)} %param.28, bf16[4,2,64,768]{3,2,1,0:T(8,128)(2,1)} %all-to-all-done), kind=kOutput, calls=%fused_computation.17 | convolution fusion | flops 3221225472 | bytes 21757952 | tf_op jit(solution)/shard_map/pecd,edf->pecf/dot_general | solution.py:166
  155.1 10.9 %fusion.13 = (bf16[4,2,64,2048]{3,2,0,1:T(8,128)(2,1)}, bf16[4,2,64,2048]{3,2,0,1:T(8,128)(2,1)}, bf16[4,2,64,2048]{3,2,0,1:T(8,128)(2,1)}) fusion(f32[4,2,64,4096]{3,2,0,1:T(8,128)} %fusion.4, bf16[2,2048,768]{2,1,0:T(8,128)(2,1)} %param.29, bf16[4,2,64,768]{3,2,1,0:T(8,128)(2,1)} %all-to-all-done.2), kind=kOutput, calls=%fused_computation.27 | convolution fusion | flops 1626341376 | bytes 21757952 | tf_op jit(solution)/shard_map/pecd,efd->pecf/dot_general | solution.py:229
  166.0 10.2 %fusion.28 = bf16[4,2,64,768]{3,2,0,1:T(8,128)(2,1)} fusion(bf16[2,768,4096]{2,1,0:T(8,128)(2,1)} %param.28, bf16[4,2,64,2048]{3,2,0,1:T(8,128)(2,1)} %get-tuple-element.70, bf16[4,2,64,2048]{3,2,0,1:T(8,128)(2,1)} %get-tuple-element.69), kind=kOutput, calls=%fused_computation.52 | convolution fusion | flops 3230007296 | bytes 17563648 | tf_op jit(solution)/shard_map/pecf,edf->pecd/dot_general | solution.py:239
  178.3 4.2 all-to-all-start.3
  182.5 5.2 fusion.31
  188.6 5.5 all-to-all-done.3
  194.1 4.2 all-to-all-start.1
  198.6 3.2 fusion.104
  203.1 4.3 gather_fusion.6
  207.4 2.9 reshape.509
  210.4 4.3 gather_fusion.3
  214.7 3.0 reshape.508
  217.6 7.4 select_reduce_fusion
  225.1 4.3 multiply_reduce_fusion.1
  234.5 2.5 multiply_reduce_fusion.3
  242.0 3.8 fusion.40
  245.8 2.3 multiply_reduce_fusion
  253.9 2.2 scatter_custom_fusion.3
  258.2 4.1 fusion.78
  264.3 6.3 bitcast_convert_fusion.1
  270.8 10.5 %bitcast_convert_fusion = bf16[2,768,4096]{2,1,0:T(8,128)(2,1)} fusion(bf16[4,2,64,768]{3,2,1,0:T(8,128)(2,1)} %all-to-all-done, bf16[4,2,64,2048]{3,2,0,1:T(8,128)(2,1)} %get-tuple-element.70, bf16[4,2,64,2048]{3,2,0,1:T(8,128)(2,1)} %get-tuple-element.69), kind=kOutput, calls=%fused_computation.11 | convolution fusion | flops 3235905536 | bytes 17563648 | tf_op jit(solution)/shard_map/pecd,pecf->edf/dot_general | solution.py:236
  281.4 3.8 scatter_custom_fusion.1
  285.3 4.1 fusion.54
  289.9 4.2 scatter_custom_fusion.2
  299.8 44.5 %all-reduce.2 = (f32[768]{0:T(1024)}, f32[768]{0:T(1024)S(1)}, f32[768,12]{0,1:T(8,128)}, f32[768,4]{0,1:T(4,128)S(1)}, f32[768,2]{0,1:T(2,128)}) all-reduce(f32[768]{0:T(1024)} %get-tuple-element.52, f32[768]{0:T(1024)} %get-tuple-element.48, f32[768,12]{0,1:T(8,128)} %fusion.106, ...), channel_id=1, replica_groups=mesh['dp'=8,'expert'=4] {'dp','expert'}, use_global_device_ids=true, to_apply=%region_33.34 | all-reduce | flops 15360 | bytes 122880 | tf_op jit(solution)/shard_map/psum | solution.py:340
  351.1 125.4 %all-reduce.6.cloned.1.call-done = (f32[768,2304]{1,0:T(8,128)}, f32[768,768]{1,0:T(8,128)}) async-done(((f32[768,2304]{1,0:T(8,128)}, f32[768,768]{1,0:T(8,128)}), (f32[768,2304]{1,0:T(8,128)}, f32[768,768]{1,0:T(8,128)})) %all-reduce.6.cloned.1.call-update) | async-done | bytes 9437200 | tf_op jit(solution)/shard_map/psum | solution.py:340
  478.2 2.1 constant_dynamic-slice_fusion.4
  480.3 117.7 %reduce-scatter.14.cloned.1.call-done = bf16[2,256,768]{2,1,0:T(8,128)(2,1)} async-done(((bf16[2,2048,768]{2,1,0:T(8,128)(2,1)}), bf16[2,256,768]{2,1,0:T(8,128)(2,1)}) %reduce-scatter.14.cloned.1.call-update) | async-done | bytes 786448 | tf_op jit(solution)/shard_map/reduce_scatter | solution.py:247
  598.0 2.4 convert_element_type.159
  600.4 207.8 %reduce-scatter.12.cloned.1.call-done = bf16[2,96,4096]{2,1,0:T(8,128)(2,1)} async-done(((bf16[2,768,4096]{2,1,0:T(8,128)(2,1)}), bf16[2,96,4096]{2,1,0:T(8,128)(2,1)}) %reduce-scatter.12.cloned.1.call-update) | async-done | bytes 1572880 | tf_op jit(solution)/shard_map/reduce_scatter | solution.py:244
  808.2 3.4 convert_element_type.157
  811.6 26.8 %reduce-scatter.6.cloned.1.call-done = bf16[256,768]{1,0:T(8,128)(2,1)} async-done(((bf16[1024,768]{1,0:T(8,128)(2,1)}), bf16[256,768]{1,0:T(8,128)(2,1)}) %reduce-scatter.6.cloned.1.call-update) | async-done | bytes 393232 | tf_op jit(solution)/shard_map/reduce_scatter | solution.py:196
  838.4 31.1 %reduce-scatter.8.cloned.1.call-done = bf16[256,768]{1,0:T(8,128)(2,1)} async-done(((bf16[1024,768]{1,0:T(8,128)(2,1)}), bf16[256,768]{1,0:T(8,128)(2,1)}) %reduce-scatter.8.cloned.1.call-update) | async-done | bytes 393232 | tf_op jit(solution)/shard_map/reduce_scatter | solution.py:327
  (247 shorter events, 107.1 us)
Async XLA Ops:
  7.2 55.8 %copy-start = (bf16[768,2304]{1,0:T(8,128)(2,1)S(1)}, bf16[768,2304]{1,0:T(8,128)(2,1)}, u32[]{:S(2)}) copy-start(bf16[768,2304]{1,0:T(8,128)(2,1)} %param.23) | copy-start | bytes 10616836
  7.2 50.9 %all-gather.3.cloned.1.call-start = ((), (), s32[]{:S(2)}) async-start(), calls=%async_computation.9 | async-start | bytes 1966080 | tf_op jit(solution)/shard_map/all_gather | solution.py:93
  7.9 64.0 %all-gather.5.cloned.1.call-start = ((), (), s32[]{:S(2)}) async-start(), calls=%async_computation.11 | async-start | bytes 1966080 | tf_op jit(solution)/shard_map/all_gather | solution.py:202
  13.2 49.8 %copy-start.37 = (f32[768]{0:T(1024)S(1)}, f32[768]{0:T(1024)}, u32[]{:S(2)}) copy-start(f32[768]{0:T(1024)} %param.21) | copy-start | bytes 9220
  17.9 47.7 %copy-start.54 = (s32[1024]{0:T(1024)}, s32[1024]{0:T(1024)S(1)}, u32[]{:S(2)}) copy-start(s32[1024]{0:T(1024)S(1)} %pad_clamp_fusion.3) | copy-start | bytes 12292
  63.0 2.6 copy-start.40
  65.6 2.5 copy-start.13
  69.1 2.2 copy-start.21
  69.9 7.9 copy-start.44
  71.3 8.6 copy-start.50
  85.9 53.3 %all-to-all-start = ((bf16[4,2,64,768]{3,2,1,0:T(8,128)(2,1)}), bf16[4,2,64,768]{3,2,1,0:T(8,128)(2,1)}, u32[]{:S(2)}, u32[]{:S(2)}) async-start(bf16[4,2,64,768]{3,2,1,0:T(8,128)(2,1)} %bitcast.161), calls=%async_computation | async-start | bytes 1572864 | tf_op jit(solution)/shard_map/all_to_all | solution.py:165
  100.9 6.9 copy-start.43
  107.8 6.6 copy-start.55
  107.9 8.6 copy-start.47
  110.4 2.6 copy-start.18
  110.4 2.6 copy-start.19
  110.4 4.0 copy-start.3
  110.4 6.1 copy-start.9
  114.3 20.1 %copy-start.42 = (f32[256,2]{0,1:T(2,128)}, f32[256,2]{0,1:T(2,128)S(1)}, u32[]{:S(2)}) copy-start(f32[256,2]{0,1:T(2,128)S(1)} %get-tuple-element.67) | copy-start | bytes 6148
  118.7 2.5 copy-start.49
  128.6 5.8 copy-start.46
  139.2 15.9 %all-to-all-start.2 = ((bf16[4,2,64,768]{3,2,1,0:T(8,128)(2,1)}), bf16[4,2,64,768]{3,2,1,0:T(8,128)(2,1)}, u32[]{:S(2)}, u32[]{:S(2)}) async-start(bf16[4,2,64,768]{3,2,1,0:T(8,128)(2,1)} %bitcast.162), calls=%async_computation.3 | async-start | bytes 1572864 | tf_op jit(solution)/shard_map/all_to_all | solution.py:218
  178.3 15.9 %all-to-all-start.3 = ((bf16[4,2,64,768]{3,2,1,0:T(8,128)(2,1)}), bf16[4,2,64,768]{3,2,1,0:T(8,128)(2,1)}, u32[]{:S(2)}, u32[]{:S(2)}) async-start(bf16[4,2,64,768]{3,2,1,0:T(8,128)(2,1)} %copy.139), calls=%async_computation.4 | async-start | bytes 1572864 | tf_op jit(solution)/shard_map/all_to_all | solution.py:242
  194.1 16.2 %all-to-all-start.1 = ((bf16[4,2,64,768]{3,2,1,0:T(8,128)(2,1)}), bf16[4,2,64,768]{3,2,1,0:T(8,128)(2,1)}, u32[]{:S(2)}, u32[]{:S(2)}) async-start(bf16[4,2,64,768]{3,2,1,0:T(8,128)(2,1)} %copy.130), calls=%async_computation.1 | async-start | bytes 1572864 | tf_op jit(solution)/shard_map/all_to_all | solution.py:175
  198.3 4.8 copy-start.53
  198.3 151.2 %reduce-scatter.10.cloned.1.call-start = ((), (), s32[]{:S(2)}) async-start(), calls=%async_computation.13 | async-start | bytes 327680 | tf_op jit(solution)/shard_map/reduce_scatter | solution.py:333
  217.6 7.4 copy-start.17
  217.6 7.4 copy-start.20
  225.1 5.3 copy-start.48
  225.1 5.3 copy-start.52
  230.4 6.6 copy-start.4
  230.4 6.6 copy-start.5
  232.6 6.2 copy-start.16
  242.0 3.8 copy-start.2
  242.0 3.8 copy-start.23
  242.0 3.8 copy-start.25
  242.0 3.8 copy-start.39
  248.1 2.3 copy-start.27
  248.1 2.3 copy-start.29
  256.1 220.4 %all-reduce.6.cloned.1.call-start = ((), (), s32[]{:S(2)}) async-start(), calls=%async_computation.16 | async-start | bytes 18874368 | tf_op jit(solution)/shard_map/psum | solution.py:340
  256.2 2.0 copy-start.7
  258.2 4.2 copy-start.14
  258.2 4.1 copy-start.11
  258.2 4.1 copy-start.22
  264.2 333.8 %reduce-scatter.14.cloned.1.call-start = ((), (), s32[]{:S(2)}) async-start(), calls=%async_computation.15 | async-start | bytes 7077888 | tf_op jit(solution)/shard_map/reduce_scatter | solution.py:247
  270.6 537.6 %reduce-scatter.12.cloned.1.call-start = ((), (), s32[]{:S(2)}) async-start(), calls=%async_computation.14 | async-start | bytes 14155776 | tf_op jit(solution)/shard_map/reduce_scatter | solution.py:244
  281.3 557.1 %reduce-scatter.6.cloned.1.call-start = ((), (), s32[]{:S(2)}) async-start(), calls=%async_computation.10 | async-start | bytes 1966080 | tf_op jit(solution)/shard_map/reduce_scatter | solution.py:196
  285.2 584.3 %reduce-scatter.8.cloned.1.call-start = ((), (), s32[]{:S(2)}) async-start(), calls=%async_computation.12 | async-start | bytes 1966080 | tf_op jit(solution)/shard_map/reduce_scatter | solution.py:327
  (21 other events, 25.5 us)
Sparse Core Ops, SparseCore 0:
  9.6 22.3 all-gather.2
  33.5 21.0 all-gather.4
  256.2 21.7 reduce-scatter.9
  284.4 192.0 all-reduce.5
  479.9 118.0 reduce-scatter.13
  601.4 206.6 reduce-scatter.11
  811.3 27.1 reduce-scatter.5
  841.5 27.9 reduce-scatter.7
where the time goes:
time: 883 us; the launch traced here: 877 us
  waiting for transfers between devices  516 us (58%)
  local copies, waits for them, and re-layouts  98.6 us (11%)
  matrix products  93.2 us (11%)
  other arithmetic  69.5 us (8%)
  blocking collectives  55.2 us (6%)
  starting transfers between devices  28.2 us (3%)
  between operations  15.8 us (2%)
    reduce_scatter x1, waiting for transfers between devices, local(): lax.psum_scatter(up_partial.astype(jnp.bfloat16), 'dp', scatter_dimension...  208 us
    psum x1, waiting for transfers between devices, local(): lax.psum((gain_first, gain_second, in_partial, out_partial, router_partia...  125 us
    reduce_scatter x1, waiting for transfers between devices, local(): lax.psum_scatter(down_partial.astype(jnp.bfloat16), 'dp', scatter_dimensi...  118 us
    psum x1, blocking collectives, local(): lax.psum((gain_first, gain_second, in_partial, out_partial, router_partia...  44.5 us
    reduce_scatter x1, waiting for transfers between devices, local(): lax.psum_scatter(placed_x.astype(jnp.float32).astype(jnp.bfloat16), 'expe...  31.1 us
    reduce_scatter x1, waiting for transfers between devices, local(): lax.psum_scatter(placed_out.astype(jnp.float32).astype(jnp.bfloat16), 'ex...  26.8 us
  transfers between devices with their start and end apart: 12, of which 7 were waited for; matrix products, arithmetic and copies ran while one was open for 20% of the time, Pallas kernels for 0%

commit v1 on v0

v1 whole, which is shorter than its diff:
```python
import jax
import jax.numpy as jnp
from jax import lax
from jax.sharding import PartitionSpec as P

HEADS = 12

epsilon = 1e-06
rope_base = 10000.0
highest = lax.Precision.HIGHEST
low = jnp.bfloat16
wide = jnp.float32


def mm(left, right):
    return jnp.dot(left, right, preferred_element_type=wide)


def mm_tn(left, right):
    return lax.dot_general(left, right, (((0,), (0,)), ((), ())), preferred_element_type=wide)


def norm_forward(values, norm_gain):
    inverse = lax.rsqrt(jnp.mean(values * values, axis=-1, keepdims=True) + epsilon)
    unit_rows = values * inverse
    return (unit_rows * norm_gain, unit_rows, inverse)


def norm_backward(upstream, unit_rows, inverse, norm_gain):
    scaled = upstream * norm_gain
    gain_grad = jnp.sum(upstream * unit_rows, axis=0)
    back_rows = inverse * (
        scaled - unit_rows * jnp.mean(scaled * unit_rows, axis=-1, keepdims=True)
    )
    return (back_rows, gain_grad)


def rope_tables(count, half_size):
    positions = jnp.arange(count, dtype=jnp.float32)
    inverse_freq = rope_base ** (-jnp.arange(half_size, dtype=jnp.float32) / half_size)
    angles = positions[:, None] * inverse_freq[None, :]
    return (jnp.cos(angles)[:, None, :], jnp.sin(angles)[:, None, :])


def rotate(values, cosine_table, sine_table, sign):
    half_size = values.shape[-1] // 2
    first_half = values[..., :half_size]
    second_half = values[..., half_size:]
    return jnp.concatenate(
        [
            first_half * cosine_table - sign * second_half * sine_table,
            second_half * cosine_table + sign * first_half * sine_table,
        ],
        axis=-1,
    )


class Plan:
    def __init__(self):
        self.dp = lax.axis_size("dp")
        self.peers = lax.axis_size("expert")
        self.near = self.dp == 8 and self.peers == 4
        self.me = lax.axis_index("expert")
        self.row = lax.axis_index("dp")

    def flip(self, value, mask):
        return lax.ppermute(value, "expert", [(i, i ^ mask) for i in range(4)])

    def across(self, value):
        return lax.ppermute(value, "dp", [(i, i ^ 1) for i in range(8)])

    def along(self, value, step, begin, end):
        pairs = [(z * 2 + x, (z + step) * 2 + x) for z in range(begin, end) for x in range(2)]
        return lax.ppermute(value, "dp", pairs)

    def peer_order(self):
        if self.near:
            return self.me ^ jnp.array([0, 2, 1, 3], jnp.int32)
        return jnp.arange(self.peers, dtype=jnp.int32)

    def gather_peers(self, value):
        if not self.near:
            return lax.all_gather(value, "expert", axis=0)
        pair = jnp.stack([value, self.flip(value, 2)])
        return jnp.concatenate([pair, self.flip(pair, 1)], axis=0)

    def group_order(self):
        if self.near:
            z, x = self.row // 2, self.row % 2
            same = [((z - j) % 4) * 2 + x for j in range(4)]
            other = [((z - j) % 4) * 2 + 1 - x for j in range(4)]
            return jnp.stack(same + other)
        return jnp.arange(self.dp, dtype=jnp.int32)

    def gather_groups(self, value):
        if not self.near:
            every = lax.all_gather(value, "dp", axis=0)
            return [every[i] for i in range(self.dp)]
        right_1 = self.along(value, 1, 0, 3)
        left_1 = self.along(value, -1, 1, 4)
        right_2 = self.along(right_1, 1, 1, 3)
        left_2 = self.along(left_1, -1, 1, 3)
        right_3 = self.along(right_2, 1, 2, 3)
        left_3 = self.along(left_2, -1, 1, 2)
        same = [value, right_1 + left_3, right_2 + left_2, right_3 + left_1]
        return same + [self.across(block) for block in same]

    def swap_groups(self, value):
        if not self.near:
            return lax.all_to_all(value, "dp", 0, 0, tiled=True)
        parts = []
        for mask in range(8):
            part = lax.dynamic_index_in_dim(value, self.row ^ mask, 0, keepdims=False)
            if mask:
                part = lax.ppermute(part, "dp", [(i, i ^ mask) for i in range(8)])
            parts.append(part)
        return jnp.take(jnp.stack(parts), self.row ^ jnp.arange(8), axis=0)

    def sum_rows(self, partial):
        if not self.near:
            total = lax.psum(partial.astype(low).astype(wide), "expert")
            return lax.psum_scatter(total, "dp", scatter_dimension=0, tiled=True)[0]
        width = partial.shape[-1] // 4
        core, high = self.me % 2, self.me // 2
        z, x = self.row // 2, self.row % 2
        take = lax.dynamic_slice_in_dim
        keep = take(partial, core * 2 * width, 2 * width, 2)
        send = take(partial, (1 - core) * 2 * width, 2 * width, 2).astype(low)
        keep = keep + self.flip(send, 1).astype(wide)
        send = take(keep, (1 - high) * width, width, 2).astype(low)
        keep = take(keep, high * width, width, 2)
        keep = keep + self.flip(send, 2).astype(wide)
        keep = keep.reshape(4, 2, *keep.shape[1:])
        send = lax.dynamic_index_in_dim(keep, 1 - x, 1, keepdims=False).astype(low)
        keep = lax.dynamic_index_in_dim(keep, x, 1, keepdims=False)
        keep = keep + self.across(send).astype(wide)
        total = lax.dynamic_index_in_dim(keep, z, 0, keepdims=False)
        sent = keep.astype(low)
        for step in (1, 2, 3):
            part = lax.dynamic_index_in_dim(sent, (z + step) % 4, 0, keepdims=False)
            pairs = [(a * 2 + b, ((a + step) % 4) * 2 + b) for a in range(4) for b in range(2)]
            total = total + lax.ppermute(part, "dp", pairs).astype(wide)
        mine = total.astype(low)
        parts = jnp.stack([mine] + [self.flip(mine, mask) for mask in (1, 2, 3)])
        columns = jnp.take(parts, self.me ^ jnp.array([0, 2, 1, 3], jnp.int32), axis=0)
        return jnp.concatenate([columns[i] for i in range(4)], axis=-1).astype(wide)


def local(
    layer_input,
    output_grad,
    prev_logits,
    deal_order,
    routes,
    lengths,
    attention_gain,
    mixture_gain,
    attention_in,
    attention_out,
    router_weight,
    constant_mix,
    constant_value,
    expert_gate_up,
    expert_down,
):
    plan = Plan()
    tok_count = layer_input.shape[0]
    model_width = layer_input.shape[1]
    choice_count = prev_logits.shape[1]
    local_experts = expert_gate_up.shape[0]
    hidden_units = expert_down.shape[1]
    peer_count = plan.peers
    experts_all = local_experts * peer_count
    capacity = tok_count // 4
    send_rows = experts_all * capacity
    head_count = HEADS
    head_size = model_width // head_count
    half_size = head_size // 2
    score_scale = head_size ** (-0.5)
    slot_order = deal_order[0]
    iota = jnp.arange(tok_count, dtype=jnp.int32)

    group_x = plan.gather_peers(layer_input).reshape(-1, model_width)
    group_dy = plan.gather_peers(output_grad).reshape(-1, model_width)
    group_prev = plan.gather_peers(prev_logits).reshape(-1, choice_count)
    group_slots = plan.gather_peers(deal_order).reshape(-1)
    given_rows = (plan.peer_order()[:, None] * tok_count + iota[None, :]).reshape(-1)
    deal_pick = (slot_order[:, None] == given_rows[None, :]).astype(low)
    own_rows = plan.me * tok_count + iota
    home_pick = (group_slots[None, :] == own_rows[:, None]).astype(low)

    dealt_rows = mm(deal_pick, group_x)
    dy_low = mm(deal_pick, group_dy).astype(low)
    prev_dealt = mm(deal_pick, group_prev)
    grad_out = dy_low.astype(wide)

    choices = jnp.arange(choice_count, dtype=jnp.int32)
    route_onehot = (routes[..., None] == choices).astype(wide)
    hits = jnp.sum(route_onehot, axis=1)
    earlier = mm((iota[None, :] < iota[:, None]).astype(low), hits.astype(low))
    rank = jnp.sum(route_onehot * earlier[:, None, :], axis=-1).astype(jnp.int32)
    is_ffn = routes < experts_all
    target = jnp.where(is_ffn, routes * capacity + rank, send_rows)
    places = jnp.arange(send_rows, dtype=jnp.int32)
    pick_0 = target[:, 0][:, None] == places[None, :]
    pick_1 = target[:, 1][:, None] == places[None, :]
    both_pick = (pick_0 | pick_1).astype(low)

    def to_experts(rows):
        outgoing = mm_tn(both_pick, rows).astype(low)
        outgoing = outgoing.reshape(peer_count, local_experts * capacity, model_width)
        incoming = lax.all_to_all(outgoing, "expert", split_axis=0, concat_axis=0, tiled=True)
        incoming = incoming.reshape(peer_count, local_experts, capacity, model_width)
        return incoming.transpose(1, 0, 2, 3).reshape(local_experts, -1, model_width)

    def from_experts(rows):
        rows = rows.reshape(local_experts, peer_count, capacity, model_width).transpose(1, 0, 2, 3)
        rows = rows.reshape(peer_count, local_experts * capacity, model_width)
        rows = lax.all_to_all(rows, "expert", split_axis=0, concat_axis=0, tiled=True)
        return rows.reshape(send_rows, model_width)

    dy_in = to_experts(dy_low)
    dy_blocks = plan.gather_groups(dy_in)

    normed_first, unit_first, inverse_first = norm_forward(dealt_rows, attention_gain)
    first_low = normed_first.astype(low)
    projected = mm(first_low, attention_in)
    projected = projected.reshape(tok_count, 3, head_count, head_size)
    cosine_table, sine_table = rope_tables(tok_count, half_size)
    query_rot = rotate(projected[:, 0], cosine_table, sine_table, 1.0).astype(low)
    key_rot = rotate(projected[:, 1], cosine_table, sine_table, 1.0).astype(low)
    value_low = projected[:, 2].astype(low)
    allowed = (iota[None, :] <= iota[:, None]) & (iota[None, :] < lengths[0])
    raw_scores = (
        jnp.einsum("ihd,jhd->hij", query_rot, key_rot, preferred_element_type=wide) * score_scale
    )
    scores = jnp.where(allowed[None], raw_scores, -jnp.inf)
    score_peak = jnp.max(scores, axis=-1, keepdims=True)
    exp_scores = jnp.exp(scores - score_peak)
    score_probs = exp_scores / jnp.sum(exp_scores, axis=-1, keepdims=True)
    probs_low = score_probs.astype(low)
    attended = (
        jnp.einsum("hij,jhd->ihd", probs_low, value_low, preferred_element_type=wide)
        .astype(low)
        .reshape(tok_count, model_width)
    )
    residual = dealt_rows + mm(attended, attention_out)
    normed_second, unit_second, inverse_second = norm_forward(residual, mixture_gain)
    second_low = normed_second.astype(low)

    x_in = to_experts(second_low)
    x_blocks = plan.gather_groups(x_in)

    logits = mm(second_low, router_weight) + prev_dealt
    picked = jnp.sum(route_onehot * logits[:, None, :], axis=-1)
    gate_values = jax.nn.softmax(picked, axis=-1)
    gates_sent = jnp.sum(
        jnp.where(pick_0, gate_values[:, 0:1], 0.0) + jnp.where(pick_1, gate_values[:, 1:2], 0.0), axis=0
    )
    gates_all = lax.all_gather(gates_sent, ("dp", "expert"), axis=0)
    mix_logits = mm(second_low, constant_mix).reshape(tok_count, 2, 2)
    mix_weights = jax.nn.softmax(mix_logits, axis=-1)
    const_rows = constant_value.astype(wide).T
    const_out = (
        mix_weights[:, :, 0:1] * normed_second[:, None, :]
        + mix_weights[:, :, 1:2] * const_rows[None]
    )

    def expert_forward(rows, gate_up_weight):
        gate_up = jnp.einsum("erd,edf->erf", rows, gate_up_weight, preferred_element_type=wide)
        width = gate_up_weight.shape[-1] // 2
        return gate_up[..., :width], gate_up[..., width:]

    def expert_back(gate_part, up_part, dy_rows, down_weight):
        sigmoid_gate = jax.nn.sigmoid(gate_part)
        grad_inner = jnp.einsum("erd,efd->erf", dy_rows, down_weight, preferred_element_type=wide)
        gate_back = grad_inner * up_part * sigmoid_gate * (1.0 + gate_part * (1.0 - sigmoid_gate))
        return jnp.concatenate([gate_back, grad_inner * gate_part * sigmoid_gate], axis=-1)

    gate_part, up_part = expert_forward(x_in, expert_gate_up)
    inner_low = (jax.nn.silu(gate_part) * up_part).astype(low)
    produced = jnp.einsum("erf,efd->erd", inner_low, expert_down, preferred_element_type=wide)
    returned = from_experts(produced.astype(low))
    back_gate_up = expert_back(gate_part, up_part, dy_in, expert_down).astype(low)
    row_grads = jnp.einsum("erf,edf->erd", back_gate_up, expert_gate_up, preferred_element_type=wide)
    row_grads = from_experts(row_grads.astype(low))

    pick_0_low, pick_1_low = pick_0.astype(low), pick_1.astype(low)
    route_out = jnp.stack([mm(pick_0_low, returned), mm(pick_1_low, returned)], axis=1)
    copy_mask = routes == experts_all + 1
    const_mask = routes[..., None] == (experts_all + 2 + jnp.arange(2, dtype=jnp.int32))
    branch = (
        route_out
        + jnp.where(copy_mask[..., None], normed_second[:, None, :], 0.0)
        + jnp.where(const_mask[..., 0:1], const_out[:, 0][:, None, :], 0.0)
        + jnp.where(const_mask[..., 1:2], const_out[:, 1][:, None, :], 0.0)
    )
    output = residual + jnp.sum(gate_values[..., None] * branch, axis=1)
    group_out = plan.gather_peers(output.astype(low)).reshape(-1, model_width)
    out_rows = mm(home_pick, group_out).astype(low)

    grad_gate = jnp.sum(branch * grad_out[:, None, :], axis=-1)
    grad_picked = gate_values * (
        grad_gate - jnp.sum(gate_values * grad_gate, axis=-1, keepdims=True)
    )
    grad_logits = jnp.sum(route_onehot * grad_picked[..., None], axis=1)
    expert_input_grad = gate_values[:, 0:1] * mm(pick_0_low, row_grads) + gate_values[
        :, 1:2
    ] * mm(pick_1_low, row_grads)
    const_weight = jnp.sum(jnp.where(const_mask, gate_values[..., None], 0.0), axis=1)
    copy_weight = jnp.sum(jnp.where(copy_mask, gate_values, 0.0), axis=1)
    along_normed = jnp.sum(grad_out * normed_second, axis=-1)
    along_value = mm(dy_low, constant_value)
    grad_mix = jnp.stack(
        [const_weight * along_normed[:, None], const_weight * along_value], axis=-1
    )
    grad_mixlog = mix_weights * (grad_mix - jnp.sum(mix_weights * grad_mix, axis=-1, keepdims=True))
    grad_mixlog = grad_mixlog.reshape(tok_count, 4)
    second_wide = second_low.astype(wide)
    narrow = jnp.concatenate([grad_logits, grad_mixlog], axis=1)
    narrow_grad = jnp.dot(second_wide.T, narrow, precision=highest)
    value_grad = jnp.dot(grad_out.T, const_weight * mix_weights[:, :, 1], precision=highest)
    direct_scale = copy_weight + jnp.sum(const_weight * mix_weights[:, :, 0], axis=1)
    narrow_weight = jnp.concatenate([router_weight, constant_mix], axis=1).astype(wide)
    grad_second = (
        direct_scale[:, None] * grad_out
        + expert_input_grad
        + jnp.dot(narrow, narrow_weight.T, precision=highest)
    )
    back_second, gain_second = norm_backward(grad_second, unit_second, inverse_second, mixture_gain)
    grad_residual = grad_out + back_second

    grad_attn = grad_residual.astype(low)
    out_partial = mm_tn(attended, grad_attn)
    grad_attended = lax.dot_general(
        grad_attn, attention_out, (((1,), (1,)), ((), ())), preferred_element_type=wide
    )
    grad_attended = grad_attended.astype(low).reshape(tok_count, head_count, head_size)
    grad_value = jnp.einsum("hij,ihd->jhd", probs_low, grad_attended, preferred_element_type=wide)
    grad_probs = jnp.einsum("ihd,jhd->hij", grad_attended, value_low, preferred_element_type=wide)
    grad_scores = (
        score_probs * (grad_probs - jnp.sum(score_probs * grad_probs, axis=-1, keepdims=True))
    ).astype(low)
    grad_query = (
        jnp.einsum("hij,jhd->ihd", grad_scores, key_rot, preferred_element_type=wide) * score_scale
    )
    grad_key = (
        jnp.einsum("hij,ihd->jhd", grad_scores, query_rot, preferred_element_type=wide)
        * score_scale
    )
    grad_qkv = jnp.stack(
        [
            rotate(grad_query, cosine_table, sine_table, -1.0),
            rotate(grad_key, cosine_table, sine_table, -1.0),
            grad_value,
        ],
        axis=1,
    )
    grad_qkv = grad_qkv.reshape(tok_count, 3 * model_width).astype(low)
    in_partial = mm_tn(first_low, grad_qkv)
    grad_first = lax.dot_general(
        grad_qkv, attention_in, (((1,), (1,)), ((), ())), preferred_element_type=wide
    )
    back_first, gain_first = norm_backward(grad_first, unit_first, inverse_first, attention_gain)
    grad_dealt = grad_residual + back_first

    group_back = plan.gather_peers(grad_dealt.astype(low)).reshape(-1, model_width)
    input_rows = mm(home_pick, group_back).astype(low)
    group_logits = plan.gather_peers(grad_logits.astype(low)).reshape(-1, choice_count)
    prev_rows = mm(home_pick, group_logits).astype(low)

    share_rows = model_width // plan.dp
    matrices = jnp.concatenate([in_partial, out_partial], axis=1).reshape(plan.dp, share_rows, -1)
    narrow_all = jnp.concatenate(
        [narrow_grad, value_grad, gain_first[:, None], gain_second[:, None]], axis=1
    )
    narrow_count = narrow_all.shape[1]
    flat = narrow_all.reshape(plan.dp, 1, share_rows * narrow_count)
    flat = jnp.pad(flat, ((0, 0), (0, 7), (0, 4 * model_width - share_rows * narrow_count)))
    total = plan.sum_rows(jnp.concatenate([matrices, flat], axis=1))
    in_grad = total[:share_rows, : 3 * model_width]
    out_grad = total[:share_rows, 3 * model_width :]
    narrow_sum = total[share_rows, : share_rows * narrow_count].reshape(share_rows, narrow_count)

    share = hidden_units // plan.dp
    first_unit = plan.row * share
    gate_weight = lax.dynamic_slice_in_dim(expert_gate_up, first_unit, share, 2)
    up_weight = lax.dynamic_slice_in_dim(expert_gate_up, hidden_units + first_unit, share, 2)
    down_weight = lax.dynamic_slice_in_dim(expert_down, first_unit, share, 1)
    x_all = jnp.concatenate(x_blocks, axis=1)
    dy_all = jnp.concatenate(dy_blocks, axis=1)
    gates_all = gates_all.reshape(plan.dp, peer_count, peer_count, local_experts, capacity)
    gates_all = lax.dynamic_index_in_dim(gates_all, plan.me, 2, keepdims=False)
    gates_all = jnp.take(gates_all, plan.group_order(), axis=0)
    gates_all = gates_all.transpose(2, 0, 1, 3).reshape(local_experts, -1)[..., None]
    gate_part, up_part = expert_forward(x_all, jnp.concatenate([gate_weight, up_weight], axis=-1))
    gated_inner = (jax.nn.silu(gate_part) * up_part * gates_all).astype(low)
    down_sum = jnp.einsum("erf,erd->efd", gated_inner, dy_all, preferred_element_type=wide)
    back_all = (expert_back(gate_part, up_part, dy_all, down_weight) * gates_all).astype(low)
    up_partial = jnp.einsum("erd,erf->edf", x_all, back_all, preferred_element_type=wide)
    up_partial = up_partial.astype(low).reshape(local_experts, plan.dp, share_rows, 2 * share)
    swapped = plan.swap_groups(up_partial.transpose(1, 0, 2, 3))
    swapped = swapped.reshape(plan.dp, local_experts, share_rows, 2, share)
    gate_up_sum = swapped.transpose(1, 2, 3, 0, 4).reshape(local_experts, share_rows, -1)
    return (
        out_rows,
        input_rows,
        prev_rows,
        narrow_sum[:, choice_count + 6],
        narrow_sum[:, choice_count + 7],
        in_grad,
        out_grad,
        narrow_sum[:, :choice_count],
        narrow_sum[:, choice_count : choice_count + 4],
        narrow_sum[:, choice_count + 4 : choice_count + 6],
        gate_up_sum.astype(wide),
        down_sum,
    )


def solution(mesh):
    in_specs = (
        P(("dp", "expert"), None),
        P(("dp", "expert"), None),
        P(("dp", "expert"), None),
        P("dp", "expert"),
        P(("dp", "expert"), None),
        P(("dp", "expert")),
        P(),
        P(),
        P(),
        P(),
        P(),
        P(),
        P(),
        P("expert", None, None),
        P("expert", None, None),
    )
    out_specs = (
        P(("dp", "expert"), None),
        P(("dp", "expert"), None),
        P(("dp", "expert"), None),
        P("dp"),
        P("dp"),
        P("dp", None),
        P("dp", None),
        P("dp", None),
        P("dp", None),
        P("dp", None),
        P("expert", "dp", None),
        P("expert", "dp", None),
    )
    return jax.shard_map(local, mesh=mesh, in_specs=in_specs, out_specs=out_specs, check_vma=False)
```

time: 883 us -> 588 us (0.67)
  waiting for transfers between devices: 516 us -> 153 us
  starting transfers between devices: 28.2 us -> 82.6 us
  matrix products: 93.2 us -> 125 us
  local copies, waits for them, and re-layouts: 98.6 us -> 85.7 us
  between operations: 15.8 us -> 3.12 us
  other arithmetic: 69.5 us -> 82 us
  blocking collectives: 55.2 us -> 45.5 us
    reduce_scatter x5 -> x0, waiting for transfers between devices: 383 us -> none  [the longest x1 208 us: local(): lax.psum_scatter(up_partial.astype(jnp.bfloat16), 'dp', scatter_dimension...]
    ppermute x0 -> x50, waiting for transfers between devices: none -> 153 us  [the longest x9 81.9 us: across(): return lax.ppermute(value, 'dp', [(i, i ^ 1) for i in range(8)])]
    psum x1 -> x0, waiting for transfers between devices: 125 us -> none  [local(): lax.psum((gain_first, gain_second, in_partial, out_partial, router_partia...]
    ppermute x0 -> x50, starting transfers between devices: none -> 65.6 us  [the longest x7 25.4 us: swap_groups(): part = lax.ppermute(part, 'dp', [(i, i ^ mask) for i in range(8)])]
    psum x1 -> x0, blocking collectives: 44.5 us -> none  [local(): lax.psum((gain_first, gain_second, in_partial, out_partial, router_partia...]
    all_gather x1, blocking collectives: 10.7 us -> 45.5 us  [local(): gates_all = lax.all_gather(gates_sent, ('dp', 'expert'), axis=0)]
    dot_general x23 -> x35, matrix products: 87.5 us -> 117 us  [the longest x16 20.8 us: mm(): return jnp.dot(left, right, preferred_element_type=wide)]
    gather x8 -> x4, local copies, waits for them, and re-layouts: 28.3 us -> 6.82 us  [the longest x2 4.04 us: swap_groups(): return jnp.take(jnp.stack(parts), self.row ^ jnp.arange(8), axis=0)]
  transfers between devices with their start and end apart: 12 -> 54, of which waited for: 7 -> 19; matrix products, arithmetic and copies ran while one was open for 20% -> 40% of each run, Pallas kernels for 0% -> 0%
where the time goes in v1:
time: 588 us; the launch traced here: 577 us
  waiting for transfers between devices  153 us (26%)
  matrix products  125 us (21%)
  local copies, waits for them, and re-layouts  85.7 us (15%)
  starting transfers between devices  82.6 us (14%)
  other arithmetic  82 us (14%)
  blocking collectives  45.5 us (8%)
    ppermute x9, waiting for transfers between devices, across(): return lax.ppermute(value, 'dp', [(i, i ^ 1) for i in range(8)])  81.9 us
    ppermute x12, waiting for transfers between devices, along(): return lax.ppermute(value, 'dp', pairs)  45.5 us
    all_gather x1, blocking collectives, local(): gates_all = lax.all_gather(gates_sent, ('dp', 'expert'), axis=0)  45.5 us
    unnamed x215, local copies, waits for them, and re-layouts  31.4 us
    ppermute x7, starting transfers between devices, swap_groups(): part = lax.ppermute(part, 'dp', [(i, i ^ mask) for i in range(8)])  25.4 us
    dot_general x16, matrix products, mm(): return jnp.dot(left, right, preferred_element_type=wide)  20.8 us
    dot_general x2, matrix products, expert_back(): jnp.einsum('erd,efd->erf', dy_rows, down_weight, preferred_element_type=w...  20.3 us
    dot_general x2, matrix products, expert_forward(): jnp.einsum('erd,edf->erf', rows, gate_up_weight, preferred_element_type=w...  19.4 us
  transfers between devices with their start and end apart: 54, of which 19 were waited for; matrix products, arithmetic and copies ran while one was open for 40% of the time, Pallas kernels for 0%

profile of v1, /device:TPU:0, one launch (start us, length us, event | category | flops | bytes accessed | tf_op | source)
XLA Modules:
  0.0 576.8 jit_solution(6663746456593785836)
XLA Ops:
  0.7 3.1 collective-permute-start.2
  18.6 2.6 constant_dynamic-slice_fusion.2
  47.1 4.1 fusion.141
  51.2 2.7 convolution_convert_fusion.4
  74.6 4.2 all-to-all-start
  86.7 45.5 %all-gather.1 = f32[32,1,512]{2,1,0:T(1,128)} all-gather(f32[1,1,512]{2,1,0:T(1,128)S(1)} %bitcast.349), channel_id=2, replica_groups=mesh['dp'=8,'expert'=4] {'dp','expert'}, dimensions={0}, use_global_device_ids=true | all-gather | bytes 67584 | tf_op jit(solution)/shard_map/all_gather | solution.py:260
  145.6 4.4 all-to-all-start.2
  152.0 10.4 %fusion.143 = f32[2,256,4096]{2,1,0:T(8,128)} fusion(bf16[2,256,768]{2,1,0:T(8,128)(2,1)S(1)} %bitcast.271, bf16[2,768,4096]{2,1,0:T(8,128)(2,1)} %param.30), kind=kOutput, calls=%fused_computation.319 | convolution fusion | flops 3221225472 | bytes 21757952 | tf_op jit(solution)/shard_map/erd,edf->erf/dot_general | solution.py:270
  163.8 7.5 %fusion.36 = bf16[2,256,768]{2,1,0:T(8,128)(2,1)S(1)} fusion(bf16[2,2048,768]{2,1,0:T(8,128)(2,1)} %param.31, f32[2,256,4096]{2,1,0:T(8,128)} %fusion.143), kind=kOutput, calls=%fused_computation.67 | convolution fusion | flops 1617297408 | bytes 15466496 | tf_op jit(solution)/shard_map/erf,efd->erd/dot_general | solution.py:282
  171.4 9.0 %multiply_convert_fusion.2 = (bf16[2,256,2048]{2,1,0:T(8,128)(2,1)}, bf16[2,256,2048]{2,1,0:T(8,128)(2,1)}) fusion(f32[2,256,4096]{2,1,0:T(8,128)S(1)} %bitcast.268, bf16[2,256,768]{2,1,0:T(8,128)(2,1)S(1)} %bitcast.288, bf16[2,2048,768]{2,1,0:T(8,128)(2,1)} %param.31), kind=kOutput, calls=%fused_computation.22 | convolution fusion | flops 1624244224 | bytes 19660800 | tf_op jit(solution)/shard_map/erd,efd->erf/dot_general | solution.py:276
  181.4 4.2 all-to-all-start.1
  185.6 10.2 %fusion.37 = bf16[2,256,768]{2,1,0:T(8,128)(2,1)} fusion(bf16[2,768,4096]{2,1,0:T(8,128)(2,1)} %param.30, bf16[2,256,2048]{2,1,0:T(8,128)(2,1)} %get-tuple-element.99, bf16[2,256,2048]{2,1,0:T(8,128)(2,1)} %get-tuple-element.98), kind=kOutput, calls=%fused_computation.68 | convolution fusion | flops 3230007296 | bytes 17563648 | tf_op jit(solution)/shard_map/erf,edf->erd/dot_general | solution.py:285
  197.8 4.2 all-to-all-start.3
  219.2 2.4 convolution_bitcast_fusion.1
  223.3 2.9 multiply_reduce_fusion.1
  234.5 2.7 fusion.53
  245.3 2.7 multiply_reduce_fusion.4
  248.0 4.2 fusion.136
  254.8 8.2 %pad_maximum_fusion = f32[768,3072]{1,0:T(8,128)} fusion(f32[768,768]{1,0:T(8,128)S(1)} %copy-done.19, f32[768,2304]{1,0:T(8,128)} %fusion.136), kind=kLoop, calls=%fused_computation.6 | loop fusion | flops 2359296 | bytes 18874368 | tf_op jit(solution)/shard_map/concatenate | solution.py:373
  263.0 4.7 select_maximum_fusion
  273.6 5.3 collective-permute-done.10
  280.2 4.9 collective-permute-start.33
  287.4 5.5 collective-permute-done.25
  296.6 5.6 collective-permute-done.33
  306.6 8.7 %collective-permute-done.35 = bf16[2,256,768]{2,1,0:T(8,128)(2,1)S(1)} collective-permute-done((bf16[2,256,768]{2,1,0:T(8,128)(2,1)}, bf16[2,256,768]{2,1,0:T(8,128)(2,1)S(1)}, u32[]{:S(2)}, u32[]{:S(2)}) %collective-permute-start.35) | collective-permute-done | bytes 786464 | tf_op jit(solution)/shard_map/ppermute | solution.py:74
  315.3 14.3 %collective-permute-done.26 = bf16[2,256,768]{2,1,0:T(8,128)(2,1)S(1)} collective-permute-done((bf16[2,256,768]{2,1,0:T(8,128)(2,1)S(1)}, bf16[2,256,768]{2,1,0:T(8,128)(2,1)S(1)}, u32[]{:S(2)}, u32[]{:S(2)}) %collective-permute-start.26) | collective-permute-done | bytes 786464 | tf_op jit(solution)/shard_map/ppermute | solution.py:74
  337.2 11.4 %collective-permute-done.36 = bf16[2,256,768]{2,1,0:T(8,128)(2,1)S(1)} collective-permute-done((bf16[2,256,768]{2,1,0:T(8,128)(2,1)S(1)}, bf16[2,256,768]{2,1,0:T(8,128)(2,1)S(1)}, u32[]{:S(2)}, u32[]{:S(2)}) %collective-permute-start.36) | collective-permute-done | bytes 786464 | tf_op jit(solution)/shard_map/ppermute | solution.py:74
  353.7 2.5 constant_dynamic-update-slice_fusion.12
  360.2 11.3 %collective-permute-done.30 = bf16[2,256,768]{2,1,0:T(8,128)(2,1)S(1)} collective-permute-done((bf16[2,256,768]{2,1,0:T(8,128)(2,1)S(1)}, bf16[2,256,768]{2,1,0:T(8,128)(2,1)S(1)}, u32[]{:S(2)}, u32[]{:S(2)}) %collective-permute-start.30) | collective-permute-done | bytes 786464 | tf_op jit(solution)/shard_map/ppermute | solution.py:70
  372.7 15.7 %collective-permute-done.31 = bf16[2,256,768]{2,1,0:T(8,128)(2,1)S(1)} collective-permute-done((bf16[2,256,768]{2,1,0:T(8,128)(2,1)S(1)}, bf16[2,256,768]{2,1,0:T(8,128)(2,1)S(1)}, u32[]{:S(2)}, u32[]{:S(2)}) %collective-permute-start.31) | collective-permute-done | bytes 786464 | tf_op jit(solution)/shard_map/ppermute | solution.py:70
  390.1 15.1 %collective-permute-done.32 = bf16[2,256,768]{2,1,0:T(8,128)(2,1)S(1)} collective-permute-done((bf16[2,256,768]{2,1,0:T(8,128)(2,1)S(1)}, bf16[2,256,768]{2,1,0:T(8,128)(2,1)S(1)}, u32[]{:S(2)}, u32[]{:S(2)}) %collective-permute-start.32) | collective-permute-done | bytes 786464 | tf_op jit(solution)/shard_map/ppermute | solution.py:70
  406.2 15.9 %collective-permute-done.40 = bf16[2,256,768]{2,1,0:T(8,128)(2,1)S(1)} collective-permute-done((bf16[2,256,768]{2,1,0:T(8,128)(2,1)S(1)}, bf16[2,256,768]{2,1,0:T(8,128)(2,1)S(1)}, u32[]{:S(2)}, u32[]{:S(2)}) %collective-permute-start.40) | collective-permute-done | bytes 786464 | tf_op jit(solution)/shard_map/ppermute | solution.py:70
  423.0 15.9 %collective-permute-done.41 = bf16[2,256,768]{2,1,0:T(8,128)(2,1)S(1)} collective-permute-done((bf16[2,256,768]{2,1,0:T(8,128)(2,1)S(1)}, bf16[2,256,768]{2,1,0:T(8,128)(2,1)S(1)}, u32[]{:S(2)}, u32[]{:S(2)}) %collective-permute-start.41) | collective-permute-done | bytes 786464 | tf_op jit(solution)/shard_map/ppermute | solution.py:70
  439.9 9.0 %fusion.29 = f32[2,2048,512]{1,2,0:T(8,128)} fusion(bf16[2,2048,768]{2,1,0:T(8,128)(2,1)} %constant_dynamic-update-slice_fusion, bf16[2,768,256]{1,2,0:T(8,128)(2,1)S(1)} %copy-done.30, bf16[2,768,256]{1,2,0:T(8,128)(2,1)S(1)} %copy-done.31), kind=kOutput, calls=%fused_computation.56 | convolution fusion | flops 3224371200 | bytes 16252928 | tf_op jit(solution)/shard_map/erd,edf->erf/dot_general | solution.py:270
  448.9 3.5 collective-permute-done.42
  453.3 11.3 %add_multiply_fusion = (f32[2,2048,256]{1,2,0:T(8,128)}, f32[2,2048,256]{1,2,0:T(8,128)}) fusion(f32[2,2048,512]{1,2,0:T(8,128)} %fusion.29, bf16[2,2048,768]{2,1,0:T(8,128)(2,1)} %constant_dynamic-update-slice_fusion.8, bf16[2,2048,768]{2,1,0:T(8,128)(2,1)} %param.31, s32[]{:T(128)S(6)} %select_n.241), kind=kOutput, calls=%fused_computation.19 | convolution fusion | flops 1622147072 | bytes 23855108 | tf_op jit(solution)/shard_map/erd,efd->erf/dot_general | solution.py:276
  464.6 9.5 %fusion.12 = bf16[2,768,512]{2,1,0:T(8,128)(2,1)S(1)} fusion(bf16[2,2048,768]{2,1,0:T(8,128)(2,1)} %constant_dynamic-update-slice_fusion, f32[2,2048,256]{1,2,0:T(8,128)} %get-tuple-element.95, f32[2,2048,256]{1,2,0:T(8,128)} %get-tuple-element.94, f32[2,2048]{1,0:T(2,128)S(1)} %copy-done.76), kind=kOutput, calls=%fused_computation.36 | convolution fusion | flops 3228303360 | bytes 16269312 | tf_op jit(solution)/shard_map/erd,erf->edf/dot_general | solution.py:400
  474.6 8.4 %fusion.11 = f32[2,256,768]{2,1,0:T(8,128)} fusion(bf16[2,2048,768]{2,1,0:T(8,128)(2,1)} %constant_dynamic-update-slice_fusion.8, f32[2,2048,512]{1,2,0:T(8,128)} %fusion.29, f32[2,2048]{1,0:T(2,128)S(1)} %copy-done.76), kind=kOutput, calls=%fused_computation.35 | convolution fusion | flops 1617952768 | bytes 16269312 | tf_op jit(solution)/shard_map/erf,erd->efd/dot_general | solution.py:398
  483.0 11.5 %collective-permute-start.44 = (bf16[2,96,512]{2,1,0:T(8,128)(2,1)S(1)}, bf16[2,96,512]{2,1,0:T(8,128)(2,1)S(1)}, u32[]{:S(2)}, u32[]{:S(2)}) collective-permute-start(bf16[2,96,512]{2,1,0:T(8,128)(2,1)S(1)} %get-tuple-element.107), channel_id=1, source_target_pairs={{0,8},{4,12},{8,0},{12,4},{16,24},{20,28},{24,16},{28,20},{1,9},{5... | collective-permute-start | bytes 589832 | tf_op jit(solution)/shard_map/ppermute | solution.py:115
  495.5 5.3 collective-permute-start.46
  503.9 5.0 collective-permute-start.48
  515.3 8.1 %collective-permute-done.46 = bf16[2,96,512]{2,1,0:T(8,128)(2,1)S(1)} collective-permute-done((bf16[2,96,512]{2,1,0:T(8,128)(2,1)S(1)}, bf16[2,96,512]{2,1,0:T(8,128)(2,1)S(1)}, u32[]{:S(2)}, u32[]{:S(2)}) %collective-permute-start.46) | collective-permute-done | bytes 196640 | tf_op jit(solution)/shard_map/ppermute | solution.py:115
  524.1 2.9 collective-permute-done.47
  528.4 4.5 collective-permute-done.16
  541.1 5.8 collective-permute-done.18
  549.9 2.8 convert_bitcast_fusion
  552.7 3.5 copy.181
  556.2 4.6 reshape.799
  (458 shorter events, 206.1 us)
Async XLA Ops:
  0.7 28.0 %collective-permute-start.2 = (bf16[256,768]{1,0:T(8,128)(2,1)}, bf16[256,768]{1,0:T(8,128)(2,1)}, u32[]{:S(2)}, u32[]{:S(2)}) collective-permute-start(bf16[256,768]{1,0:T(8,128)(2,1)} %param.17), channel_id=1, source_target_pairs={{0,2},{1,3},{2,0},{3,1},{4,6},{5,7},{6,4},{7,5},{8,10},{9,11},{10,... | collective-permute-start | bytes 1179656 | tf_op jit(solution)/shard_map/ppermute | solution.py:67
  3.7 34.5 %collective-permute-start.8 = (bf16[256,768]{1,0:T(8,128)(2,1)}, bf16[256,768]{1,0:T(8,128)(2,1)}, u32[]{:S(2)}, u32[]{:S(2)}) collective-permute-start(bf16[256,768]{1,0:T(8,128)(2,1)} %param.18), channel_id=1, source_target_pairs={{0,2},{1,3},{2,0},{3,1},{4,6},{5,7},{6,4},{7,5},{8,10},{9,11},{10,... | collective-permute-start | bytes 1179656 | tf_op jit(solution)/shard_map/ppermute | solution.py:67
  3.8 31.6 %collective-permute-start.4 = (bf16[256,12]{0,1:T(8,128)(2,1)}, bf16[256,12]{0,1:T(8,128)(2,1)S(1)}, u32[]{:S(2)}, u32[]{:S(2)}) collective-permute-start(bf16[256,12]{0,1:T(8,128)(2,1)} %param.19), channel_id=1, source_target_pairs={{0,2},{1,3},{2,0},{3,1},{4,6},{5,7},{6,4},{7,5},{8,10},{9,11},{10,... | collective-permute-start | bytes 18440 | tf_op jit(solution)/shard_map/ppermute | solution.py:67
  5.7 28.4 %collective-permute-start = (s32[1,256]{1,0:T(1,128)}, s32[1,256]{1,0:T(1,128)}, u32[]{:S(2)}, u32[]{:S(2)}) collective-permute-start(s32[1,256]{1,0:T(1,128)} %param.20), channel_id=1, source_target_pairs={{0,2},{1,3},{2,0},{3,1},{4,6},{5,7},{6,4},{7,5},{8,10},{9,11},{10,... | collective-permute-start | bytes 3080 | tf_op jit(solution)/shard_map/ppermute | solution.py:67
  40.3 14.3 %collective-permute-start.9 = (bf16[2,256,768]{2,1,0:T(8,128)(2,1)}, bf16[2,256,768]{2,1,0:T(8,128)(2,1)}, u32[]{:S(2)}, u32[]{:S(2)}) collective-permute-start(bf16[2,256,768]{2,1,0:T(8,128)(2,1)} %pad_maximum_fusion.8), channel_id=1, source_target_pairs={{0,1},{1,0},{2,3},{3,2},{4,5},{5,4},{6,7},{7,6},{8,9},{9,8},{10,11... | collective-permute-start | bytes 2359304 | tf_op jit(solution)/shard_map/ppermute | solution.py:67
  74.6 70.9 %all-to-all-start = ((bf16[4,128,768]{2,1,0:T(8,128)(2,1)}), bf16[4,128,768]{2,1,0:T(8,128)(2,1)}, u32[]{:S(2)}, u32[]{:S(2)}) async-start(bf16[4,128,768]{2,1,0:T(8,128)(2,1)} %bitcast.294), calls=%async_computation | async-start | bytes 1572864 | tf_op jit(solution)/shard_map/all_to_all | solution.py:212
  145.6 16.9 %all-to-all-start.2 = ((bf16[4,128,768]{2,1,0:T(8,128)(2,1)}), bf16[4,128,768]{2,1,0:T(8,128)(2,1)}, u32[]{:S(2)}, u32[]{:S(2)}) async-start(bf16[4,128,768]{2,1,0:T(8,128)(2,1)} %bitcast.293), calls=%async_computation.2 | async-start | bytes 1572864 | tf_op jit(solution)/shard_map/all_to_all | solution.py:212
  181.4 16.5 %all-to-all-start.1 = ((bf16[4,128,768]{2,1,0:T(8,128)(2,1)}), bf16[4,128,768]{2,1,0:T(8,128)(2,1)}, u32[]{:S(2)}, u32[]{:S(2)}) async-start(bf16[4,128,768]{2,1,0:T(8,128)(2,1)} %bitcast.296), calls=%async_computation.1 | async-start | bytes 1572864 | tf_op jit(solution)/shard_map/all_to_all | solution.py:219
  197.8 23.8 %all-to-all-start.3 = ((bf16[4,128,768]{2,1,0:T(8,128)(2,1)}), bf16[4,128,768]{2,1,0:T(8,128)(2,1)}, u32[]{:S(2)}, u32[]{:S(2)}) async-start(bf16[4,128,768]{2,1,0:T(8,128)(2,1)} %bitcast.295), calls=%async_computation.3 | async-start | bytes 1572864 | tf_op jit(solution)/shard_map/all_to_all | solution.py:219
  207.4 77.7 %collective-permute-start.23 = (bf16[2,256,768]{2,1,0:T(8,128)(2,1)}, bf16[2,256,768]{2,1,0:T(8,128)(2,1)}, u32[]{:S(2)}, u32[]{:S(2)}) collective-permute-start(bf16[2,256,768]{2,1,0:T(8,128)(2,1)} %bitcast.272), channel_id=1, source_target_pairs={{0,8},{4,12},{8,16},{12,20},{16,24},{20,28},{1,9},{5,13},{9,17},{1... | collective-permute-start | bytes 2359304 | tf_op jit(solution)/shard_map/ppermute | solution.py:74
  209.7 61.0 %collective-permute-start.24 = (bf16[2,256,768]{2,1,0:T(8,128)(2,1)}, bf16[2,256,768]{2,1,0:T(8,128)(2,1)}, u32[]{:S(2)}, u32[]{:S(2)}) collective-permute-start(bf16[2,256,768]{2,1,0:T(8,128)(2,1)} %bitcast.273), channel_id=1, source_target_pairs={{8,0},{12,4},{16,8},{20,12},{24,16},{28,20},{9,1},{13,5},{17,9},{2... | collective-permute-start | bytes 2359304 | tf_op jit(solution)/shard_map/ppermute | solution.py:74
  211.0 74.8 %collective-permute-start.34 = (bf16[2,256,768]{2,1,0:T(8,128)(2,1)}, bf16[2,256,768]{2,1,0:T(8,128)(2,1)}, u32[]{:S(2)}, u32[]{:S(2)}) collective-permute-start(bf16[2,256,768]{2,1,0:T(8,128)(2,1)} %bitcast.289), channel_id=1, source_target_pairs={{8,0},{12,4},{16,8},{20,12},{24,16},{28,20},{9,1},{13,5},{17,9},{2... | collective-permute-start | bytes 2359304 | tf_op jit(solution)/shard_map/ppermute | solution.py:74
  252.2 20.3 %collective-permute-start.6 = (bf16[256,768]{1,0:T(8,128)(2,1)S(1)}, bf16[256,768]{1,0:T(8,128)(2,1)}, u32[]{:S(2)}, u32[]{:S(2)}) collective-permute-start(bf16[256,768]{1,0:T(8,128)(2,1)S(1)} %copy-done.23), channel_id=1, source_target_pairs={{0,2},{1,3},{2,0},{3,1},{4,6},{5,7},{6,4},{7,5},{8,10},{9,11},{10,... | collective-permute-start | bytes 1179656 | tf_op jit(solution)/shard_map/ppermute | solution.py:67
  254.1 13.8 %collective-permute-start.12 = (bf16[256,12]{0,1:T(8,128)(2,1)}, bf16[256,12]{0,1:T(8,128)(2,1)}, u32[]{:S(2)}, u32[]{:S(2)}) collective-permute-start(bf16[256,12]{0,1:T(8,128)(2,1)} %convert_element_type.185), channel_id=1, source_target_pairs={{0,2},{1,3},{2,0},{3,1},{4,6},{5,7},{6,4},{7,5},{8,10},{9,11},{10,... | collective-permute-start | bytes 18440 | tf_op jit(solution)/shard_map/ppermute | solution.py:67
  268.0 11.0 %collective-permute-start.10 = (bf16[256,768]{1,0:T(8,128)(2,1)S(1)}, bf16[256,768]{1,0:T(8,128)(2,1)S(1)}, u32[]{:S(2)}, u32[]{:S(2)}) collective-permute-start(bf16[256,768]{1,0:T(8,128)(2,1)S(1)} %add_convert_fusion), channel_id=1, source_target_pairs={{0,2},{1,3},{2,0},{3,1},{4,6},{5,7},{6,4},{7,5},{8,10},{9,11},{10,... | collective-permute-start | bytes 1179656 | tf_op jit(solution)/shard_map/ppermute | solution.py:67
  270.7 22.1 %collective-permute-start.25 = (bf16[2,256,768]{2,1,0:T(8,128)(2,1)}, bf16[2,256,768]{2,1,0:T(8,128)(2,1)S(1)}, u32[]{:S(2)}, u32[]{:S(2)}) collective-permute-start(bf16[2,256,768]{2,1,0:T(8,128)(2,1)} %collective-permute-done.24), channel_id=1, source_target_pairs={{8,0},{12,4},{16,8},{20,12},{9,1},{13,5},{17,9},{21,13},{10,2},{14... | collective-permute-start | bytes 2359304 | tf_op jit(solution)/shard_map/ppermute | solution.py:74
  273.5 20.6 %collective-permute-start.7 = (bf16[2,256,768]{2,1,0:T(8,128)(2,1)S(1)}, bf16[2,256,768]{2,1,0:T(8,128)(2,1)S(1)}, u32[]{:S(2)}, u32[]{:S(2)}) collective-permute-start(bf16[2,256,768]{2,1,0:T(8,128)(2,1)S(1)} %pad_maximum_fusion.7), channel_id=1, source_target_pairs={{0,1},{1,0},{2,3},{3,2},{4,5},{5,4},{6,7},{7,6},{8,9},{9,8},{10,11... | collective-permute-start | bytes 2359304 | tf_op jit(solution)/shard_map/ppermute | solution.py:67
  280.2 22.0 %collective-permute-start.33 = (bf16[2,256,768]{2,1,0:T(8,128)(2,1)S(1)}, bf16[2,256,768]{2,1,0:T(8,128)(2,1)S(1)}, u32[]{:S(2)}, u32[]{:S(2)}) collective-permute-start(bf16[2,256,768]{2,1,0:T(8,128)(2,1)S(1)} %bitcast.291), channel_id=1, source_target_pairs={{0,8},{4,12},{8,16},{12,20},{16,24},{20,28},{1,9},{5,13},{9,17},{1... | collective-permute-start | bytes 2359304 | tf_op jit(solution)/shard_map/ppermute | solution.py:74
  285.1 18.4 %collective-permute-start.27 = (bf16[2,256,768]{2,1,0:T(8,128)(2,1)}, bf16[2,256,768]{2,1,0:T(8,128)(2,1)S(1)}, u32[]{:S(2)}, u32[]{:S(2)}) collective-permute-start(bf16[2,256,768]{2,1,0:T(8,128)(2,1)} %collective-permute-done.23), channel_id=1, source_target_pairs={{8,16},{12,20},{16,24},{20,28},{9,17},{13,21},{17,25},{21,29},{10,... | collective-permute-start | bytes 2359304 | tf_op jit(solution)/shard_map/ppermute | solution.py:74
  285.8 18.5 %collective-permute-start.11 = (bf16[2,256,768]{2,1,0:T(8,128)(2,1)S(1)}, bf16[2,256,768]{2,1,0:T(8,128)(2,1)S(1)}, u32[]{:S(2)}, u32[]{:S(2)}) collective-permute-start(bf16[2,256,768]{2,1,0:T(8,128)(2,1)S(1)} %pad_maximum_fusion.9), channel_id=1, source_target_pairs={{0,1},{1,0},{2,3},{3,2},{4,5},{5,4},{6,7},{7,6},{8,9},{9,8},{10,11... | collective-permute-start | bytes 2359304 | tf_op jit(solution)/shard_map/ppermute | solution.py:67
  292.8 22.5 %collective-permute-start.35 = (bf16[2,256,768]{2,1,0:T(8,128)(2,1)}, bf16[2,256,768]{2,1,0:T(8,128)(2,1)S(1)}, u32[]{:S(2)}, u32[]{:S(2)}) collective-permute-start(bf16[2,256,768]{2,1,0:T(8,128)(2,1)} %collective-permute-done.34), channel_id=1, source_target_pairs={{8,0},{12,4},{16,8},{20,12},{9,1},{13,5},{17,9},{21,13},{10,2},{14... | collective-permute-start | bytes 2359304 | tf_op jit(solution)/shard_map/ppermute | solution.py:74
  294.1 35.5 %collective-permute-start.26 = (bf16[2,256,768]{2,1,0:T(8,128)(2,1)S(1)}, bf16[2,256,768]{2,1,0:T(8,128)(2,1)S(1)}, u32[]{:S(2)}, u32[]{:S(2)}) collective-permute-start(bf16[2,256,768]{2,1,0:T(8,128)(2,1)S(1)} %collective-permute-done.25), channel_id=1, source_target_pairs={{8,0},{12,4},{9,1},{13,5},{10,2},{14,6},{11,3},{15,7}} | collective-permute-start | bytes 2359304 | tf_op jit(solution)/shard_map/ppermute | solution.py:74
  302.2 57.1 %collective-permute-start.14 = (bf16[8,104,1536]{2,1,0:T(8,128)(2,1)S(1)}, bf16[8,104,1536]{2,1,0:T(8,128)(2,1)S(1)}, u32[]{:S(2)}, u32[]{:S(2)}) collective-permute-start(bf16[8,104,1536]{2,1,0:T(8,128)(2,1)S(1)} %dynamic-slice_convert_fusion), channel_id=1, source_target_pairs={{0,1},{1,0},{2,3},{3,2},{4,5},{5,4},{6,7},{7,6},{8,9},{9,8},{10,11... | collective-permute-start | bytes 7667720 | tf_op jit(solution)/shard_map/ppermute | solution.py:67
  303.5 30.7 %collective-permute-start.37 = (bf16[2,256,768]{2,1,0:T(8,128)(2,1)S(1)}, bf16[2,256,768]{2,1,0:T(8,128)(2,1)S(1)}, u32[]{:S(2)}, u32[]{:S(2)}) collective-permute-start(bf16[2,256,768]{2,1,0:T(8,128)(2,1)S(1)} %collective-permute-done.33), channel_id=1, source_target_pairs={{8,16},{12,20},{16,24},{20,28},{9,17},{13,21},{17,25},{21,29},{10,... | collective-permute-start | bytes 2359304 | tf_op jit(solution)/shard_map/ppermute | solution.py:74
  304.4 29.9 %collective-permute-start.28 = (bf16[2,256,768]{2,1,0:T(8,128)(2,1)S(1)}, bf16[2,256,768]{2,1,0:T(8,128)(2,1)S(1)}, u32[]{:S(2)}, u32[]{:S(2)}) collective-permute-start(bf16[2,256,768]{2,1,0:T(8,128)(2,1)S(1)} %collective-permute-done.27), channel_id=1, source_target_pairs={{16,24},{20,28},{17,25},{21,29},{18,26},{22,30},{19,27},{23,31}} | collective-permute-start | bytes 2359304 | tf_op jit(solution)/shard_map/ppermute | solution.py:74
  315.3 34.3 %collective-permute-start.29 = (bf16[2,256,768]{2,1,0:T(8,128)(2,1)S(1)}, bf16[2,256,768]{2,1,0:T(8,128)(2,1)S(1)}, u32[]{:S(2)}, u32[]{:S(2)}) collective-permute-start(bf16[2,256,768]{2,1,0:T(8,128)(2,1)S(1)} %bitcast.275), channel_id=1, source_target_pairs={{0,4},{4,0},{8,12},{12,8},{16,20},{20,16},{24,28},{28,24},{1,5},{5... | collective-permute-start | bytes 2359304 | tf_op jit(solution)/shard_map/ppermute | solution.py:70
  329.7 18.9 %collective-permute-start.36 = (bf16[2,256,768]{2,1,0:T(8,128)(2,1)S(1)}, bf16[2,256,768]{2,1,0:T(8,128)(2,1)S(1)}, u32[]{:S(2)}, u32[]{:S(2)}) collective-permute-start(bf16[2,256,768]{2,1,0:T(8,128)(2,1)S(1)} %collective-permute-done.35), channel_id=1, source_target_pairs={{8,0},{12,4},{9,1},{13,5},{10,2},{14,6},{11,3},{15,7}} | collective-permute-start | bytes 2359304 | tf_op jit(solution)/shard_map/ppermute | solution.py:74
  334.3 22.0 %collective-permute-start.39 = (bf16[2,256,768]{2,1,0:T(8,128)(2,1)S(1)}, bf16[2,256,768]{2,1,0:T(8,128)(2,1)S(1)}, u32[]{:S(2)}, u32[]{:S(2)}) collective-permute-start(bf16[2,256,768]{2,1,0:T(8,128)(2,1)S(1)} %bitcast.292), channel_id=1, source_target_pairs={{0,4},{4,0},{8,12},{12,8},{16,20},{20,16},{24,28},{28,24},{1,5},{5... | collective-permute-start | bytes 2359304 | tf_op jit(solution)/shard_map/ppermute | solution.py:70
  334.3 19.5 %collective-permute-start.38 = (bf16[2,256,768]{2,1,0:T(8,128)(2,1)S(1)}, bf16[2,256,768]{2,1,0:T(8,128)(2,1)S(1)}, u32[]{:S(2)}, u32[]{:S(2)}) collective-permute-start(bf16[2,256,768]{2,1,0:T(8,128)(2,1)S(1)} %collective-permute-done.37), channel_id=1, source_target_pairs={{16,24},{20,28},{17,25},{21,29},{18,26},{22,30},{19,27},{23,31}} | collective-permute-start | bytes 2359304 | tf_op jit(solution)/shard_map/ppermute | solution.py:74
  348.6 22.9 %collective-permute-start.30 = (bf16[2,256,768]{2,1,0:T(8,128)(2,1)S(1)}, bf16[2,256,768]{2,1,0:T(8,128)(2,1)S(1)}, u32[]{:S(2)}, u32[]{:S(2)}) collective-permute-start(bf16[2,256,768]{2,1,0:T(8,128)(2,1)S(1)} %get-tuple-element.83), channel_id=1, source_target_pairs={{0,4},{4,0},{8,12},{12,8},{16,20},{20,16},{24,28},{28,24},{1,5},{5... | collective-permute-start | bytes 2359304 | tf_op jit(solution)/shard_map/ppermute | solution.py:70
  349.7 38.7 %collective-permute-start.31 = (bf16[2,256,768]{2,1,0:T(8,128)(2,1)S(1)}, bf16[2,256,768]{2,1,0:T(8,128)(2,1)S(1)}, u32[]{:S(2)}, u32[]{:S(2)}) collective-permute-start(bf16[2,256,768]{2,1,0:T(8,128)(2,1)S(1)} %get-tuple-element.81), channel_id=1, source_target_pairs={{0,4},{4,0},{8,12},{12,8},{16,20},{20,16},{24,28},{28,24},{1,5},{5... | collective-permute-start | bytes 2359304 | tf_op jit(solution)/shard_map/ppermute | solution.py:70
  353.7 51.5 %collective-permute-start.32 = (bf16[2,256,768]{2,1,0:T(8,128)(2,1)S(1)}, bf16[2,256,768]{2,1,0:T(8,128)(2,1)S(1)}, u32[]{:S(2)}, u32[]{:S(2)}) collective-permute-start(bf16[2,256,768]{2,1,0:T(8,128)(2,1)S(1)} %get-tuple-element.79), channel_id=1, source_target_pairs={{0,4},{4,0},{8,12},{12,8},{16,20},{20,16},{24,28},{28,24},{1,5},{5... | collective-permute-start | bytes 2359304 | tf_op jit(solution)/shard_map/ppermute | solution.py:70
  356.3 65.8 %collective-permute-start.40 = (bf16[2,256,768]{2,1,0:T(8,128)(2,1)S(1)}, bf16[2,256,768]{2,1,0:T(8,128)(2,1)S(1)}, u32[]{:S(2)}, u32[]{:S(2)}) collective-permute-start(bf16[2,256,768]{2,1,0:T(8,128)(2,1)S(1)} %get-tuple-element.77), channel_id=1, source_target_pairs={{0,4},{4,0},{8,12},{12,8},{16,20},{20,16},{24,28},{28,24},{1,5},{5... | collective-permute-start | bytes 2359304 | tf_op jit(solution)/shard_map/ppermute | solution.py:70
  359.2 79.7 %collective-permute-start.41 = (bf16[2,256,768]{2,1,0:T(8,128)(2,1)S(1)}, bf16[2,256,768]{2,1,0:T(8,128)(2,1)S(1)}, u32[]{:S(2)}, u32[]{:S(2)}) collective-permute-start(bf16[2,256,768]{2,1,0:T(8,128)(2,1)S(1)} %get-tuple-element.75), channel_id=1, source_target_pairs={{0,4},{4,0},{8,12},{12,8},{16,20},{20,16},{24,28},{28,24},{1,5},{5... | collective-permute-start | bytes 2359304 | tf_op jit(solution)/shard_map/ppermute | solution.py:70
  371.5 80.9 %collective-permute-start.42 = (bf16[2,256,768]{2,1,0:T(8,128)(2,1)}, bf16[2,256,768]{2,1,0:T(8,128)(2,1)S(1)}, u32[]{:S(2)}, u32[]{:S(2)}) collective-permute-start(bf16[2,256,768]{2,1,0:T(8,128)(2,1)} %get-tuple-element.73), channel_id=1, source_target_pairs={{0,4},{4,0},{8,12},{12,8},{16,20},{20,16},{24,28},{28,24},{1,5},{5... | collective-permute-start | bytes 2359304 | tf_op jit(solution)/shard_map/ppermute | solution.py:70
  388.4 124.2 %collective-permute-start.15 = (bf16[8,104,768]{2,1,0:T(8,128)(2,1)S(1)}, bf16[8,104,768]{2,1,0:T(8,128)(2,1)S(1)}, u32[]{:S(2)}, u32[]{:S(2)}) collective-permute-start(bf16[8,104,768]{2,1,0:T(8,128)(2,1)S(1)} %dynamic-slice_convert_fusion.1), channel_id=1, source_target_pairs={{0,2},{1,3},{2,0},{3,1},{4,6},{5,7},{6,4},{7,5},{8,10},{9,11},{10,... | collective-permute-start | bytes 3833864 | tf_op jit(solution)/shard_map/ppermute | solution.py:67
  474.3 27.3 %collective-permute-start.43 = (bf16[2,96,512]{2,1,0:T(8,128)(2,1)S(1)}, bf16[2,96,512]{2,1,0:T(8,128)(2,1)S(1)}, u32[]{:S(2)}, u32[]{:S(2)}) collective-permute-start(bf16[2,96,512]{2,1,0:T(8,128)(2,1)S(1)} %get-tuple-element.108), channel_id=1, source_target_pairs={{0,4},{4,0},{8,12},{12,8},{16,20},{20,16},{24,28},{28,24},{1,5},{5... | collective-permute-start | bytes 589832 | tf_op jit(solution)/shard_map/ppermute | solution.py:115
  483.0 20.8 %collective-permute-start.44 = (bf16[2,96,512]{2,1,0:T(8,128)(2,1)S(1)}, bf16[2,96,512]{2,1,0:T(8,128)(2,1)S(1)}, u32[]{:S(2)}, u32[]{:S(2)}) collective-permute-start(bf16[2,96,512]{2,1,0:T(8,128)(2,1)S(1)} %get-tuple-element.107), channel_id=1, source_target_pairs={{0,8},{4,12},{8,0},{12,4},{16,24},{20,28},{24,16},{28,20},{1,9},{5... | collective-permute-start | bytes 589832 | tf_op jit(solution)/shard_map/ppermute | solution.py:115
  494.5 15.0 %collective-permute-start.45 = (bf16[2,96,512]{2,1,0:T(8,128)(2,1)S(1)}, bf16[2,96,512]{2,1,0:T(8,128)(2,1)S(1)}, u32[]{:S(2)}, u32[]{:S(2)}) collective-permute-start(bf16[2,96,512]{2,1,0:T(8,128)(2,1)S(1)} %get-tuple-element.106), channel_id=1, source_target_pairs={{0,12},{4,8},{8,4},{12,0},{16,28},{20,24},{24,20},{28,16},{1,13},{... | collective-permute-start | bytes 589832 | tf_op jit(solution)/shard_map/ppermute | solution.py:115
  495.5 27.8 %collective-permute-start.46 = (bf16[2,96,512]{2,1,0:T(8,128)(2,1)S(1)}, bf16[2,96,512]{2,1,0:T(8,128)(2,1)S(1)}, u32[]{:S(2)}, u32[]{:S(2)}) collective-permute-start(bf16[2,96,512]{2,1,0:T(8,128)(2,1)S(1)} %get-tuple-element.105), channel_id=1, source_target_pairs={{0,16},{4,20},{8,24},{12,28},{16,0},{20,4},{24,8},{28,12},{1,17},{... | collective-permute-start | bytes 589832 | tf_op jit(solution)/shard_map/ppermute | solution.py:115
  501.5 25.5 %collective-permute-start.47 = (bf16[2,96,512]{2,1,0:T(8,128)(2,1)S(1)}, bf16[2,96,512]{2,1,0:T(8,128)(2,1)S(1)}, u32[]{:S(2)}, u32[]{:S(2)}) collective-permute-start(bf16[2,96,512]{2,1,0:T(8,128)(2,1)S(1)} %get-tuple-element.104), channel_id=1, source_target_pairs={{0,20},{4,16},{8,28},{12,24},{16,4},{20,0},{24,12},{28,8},{1,21},{... | collective-permute-start | bytes 589832 | tf_op jit(solution)/shard_map/ppermute | solution.py:115
  503.9 23.8 %collective-permute-start.48 = (bf16[2,96,512]{2,1,0:T(8,128)(2,1)S(1)}, bf16[2,96,512]{2,1,0:T(8,128)(2,1)S(1)}, u32[]{:S(2)}, u32[]{:S(2)}) collective-permute-start(bf16[2,96,512]{2,1,0:T(8,128)(2,1)S(1)} %get-tuple-element.103), channel_id=1, source_target_pairs={{0,24},{4,28},{8,16},{12,20},{16,8},{20,12},{24,0},{28,4},{1,25},{... | collective-permute-start | bytes 589832 | tf_op jit(solution)/shard_map/ppermute | solution.py:115
  509.5 26.9 %collective-permute-start.49 = (bf16[2,96,512]{2,1,0:T(8,128)(2,1)S(1)}, bf16[2,96,512]{2,1,0:T(8,128)(2,1)S(1)}, u32[]{:S(2)}, u32[]{:S(2)}) collective-permute-start(bf16[2,96,512]{2,1,0:T(8,128)(2,1)S(1)} %get-tuple-element.102), channel_id=1, source_target_pairs={{0,28},{4,24},{8,20},{12,16},{16,12},{20,8},{24,4},{28,0},{1,29},{... | collective-permute-start | bytes 589832 | tf_op jit(solution)/shard_map/ppermute | solution.py:115
  513.0 19.9 %collective-permute-start.16 = (bf16[4,104,768]{2,1,0:T(8,128)(2,1)S(1)}, bf16[4,104,768]{2,1,0:T(8,128)(2,1)S(1)}, u32[]{:S(2)}, u32[]{:S(2)}) collective-permute-start(bf16[4,104,768]{2,1,0:T(8,128)(2,1)S(1)} %fusion.65), channel_id=1, source_target_pairs={{0,4},{4,0},{8,12},{12,8},{16,20},{20,16},{24,28},{28,24},{1,5},{5... | collective-permute-start | bytes 1916936 | tf_op jit(solution)/shard_map/ppermute | solution.py:70
  535.2 11.7 %collective-permute-start.18 = (bf16[104,768]{1,0:T(8,128)(2,1)S(1)}, bf16[104,768]{1,0:T(8,128)(2,1)S(1)}, u32[]{:S(2)}, u32[]{:S(2)}) collective-permute-start(bf16[104,768]{1,0:T(8,128)(2,1)S(1)} %get-tuple-element.127), channel_id=1, source_target_pairs={{0,16},{4,20},{8,24},{12,28},{16,0},{20,4},{24,8},{28,12},{1,17},{... | collective-permute-start | bytes 479240 | tf_op jit(solution)/shard_map/ppermute | solution.py:142
  535.4 11.5 %collective-permute-start.17 = (bf16[104,768]{1,0:T(8,128)(2,1)S(1)}, bf16[104,768]{1,0:T(8,128)(2,1)S(1)}, u32[]{:S(2)}, u32[]{:S(2)}) collective-permute-start(bf16[104,768]{1,0:T(8,128)(2,1)S(1)} %get-tuple-element.125), channel_id=1, source_target_pairs={{0,8},{4,12},{8,16},{12,20},{16,24},{20,28},{24,0},{28,4},{1,9},{5... | collective-permute-start | bytes 479240 | tf_op jit(solution)/shard_map/ppermute | solution.py:142
  548.0 12.8 %collective-permute-start.22 = (bf16[104,768]{1,0:T(8,128)(2,1)S(1)}, bf16[104,768]{1,0:T(8,128)(2,1)S(1)}, u32[]{:S(2)}, u32[]{:S(2)}) collective-permute-start(bf16[104,768]{1,0:T(8,128)(2,1)S(1)} %fusion.84), channel_id=1, source_target_pairs={{0,3},{1,2},{2,1},{3,0},{4,7},{5,6},{6,5},{7,4},{8,11},{9,10},{10,... | collective-permute-start | bytes 479240 | tf_op jit(solution)/shard_map/ppermute | solution.py:67
  548.0 12.8 %collective-permute-start.21 = (bf16[104,768]{1,0:T(8,128)(2,1)S(1)}, bf16[104,768]{1,0:T(8,128)(2,1)}, u32[]{:S(2)}, u32[]{:S(2)}) collective-permute-start(bf16[104,768]{1,0:T(8,128)(2,1)S(1)} %fusion.84), channel_id=1, source_target_pairs={{0,2},{1,3},{2,0},{3,1},{4,6},{5,7},{6,4},{7,5},{8,10},{9,11},{10,... | collective-permute-start | bytes 479240 | tf_op jit(solution)/shard_map/ppermute | solution.py:67
  (101 other events, 717.5 us)
